TPU v7x, 128 devices: a whole 4x4x4 slice. The times are simulated.
128 devices in a mesh: row: 8 (over z, x_hi), col: 16 (over x_lo, y, core).
Axes of the slice: x: 4 (x_hi: 2, x_lo: 2; x = x_hi * 2 + x_lo), y: 4, z: 4, core: 2. Of those that a mesh axis runs over, the one named last changes fastest.
Arguments:
- inverse_anc: float32 [8192, 8192], P('row', 'col'), may hold values from -25 to 25, as said below
- factor: float32 [8192, 4096], P('col', 'row'), may hold values from -0.0625 to 0.0625
- pattern: int32 [16, 8], replicated, may hold values 0 or 1
- d_inverse: float32 [4096, 512], P('row'), may hold values from -2 to 2, as said below
- jac_blocks: int32 [32768, 2], P(('row', 'col')), may hold values from 0 to 7, all different within a row; in each aligned block of 256 rows (0 to 255, 256 to 511, ...) at most 128 rows name the same one
- jac_values: float32 [32768, 2, 512], P(('row', 'col')), may hold values from -0.264 to 0.264
Outputs:
- diag_inverse: float32 [4096, 512], P('row')
- variance: float32 [32768], P(('row', 'col'))
Inputs may be any that keep to these rules, and one draw needn't show every extreme that they name: `inverse_anc`: exactly symmetric. `d_inverse`: each block exactly symmetric. `jac_blocks`: each row names 2 different panels; among the rows of one device no panel is named more than 128 times, a bound that some block reaches.
All inputs are finite; a program needn't handle non-finite values.
Results may differ from a plain program's by a relative error of at most 0.0003.
Values sent between devices are 32-bit elements; how exact they have to be, the bound alone decides.
No kernel may reach another device: no remote copies, remote signals or barrier semaphores. Data moves between devices by JAX's collectives and lax.ppermute only.
A program may use at most 128 MiB of HBM per device.

v0:
```python
import jax
import jax.numpy as jnp
from jax import lax
from jax.experimental import pallas as pl
from jax.experimental.pallas import tpu as pltpu
from jax.sharding import PartitionSpec as P


NZ, NH, NL, NY, NC = 4, 2, 2, 4, 2


def row_of(z, h):
    return (z % NZ) * NH + h


def col_of(l, y, j):
    return l * NY * NC + (y % NY) * NC + j


def z_shift(k):
    return [(row_of(z, h), row_of(z + k, h)) for z in range(NZ) for h in range(NH)]


H_SWAP = [(row_of(z, h), row_of(z, 1 - h)) for z in range(NZ) for h in range(NH)]
COLS = [(l, y, j) for l in range(NL) for y in range(NY) for j in range(NC)]


def y_shift(k, other_core):
    return [(col_of(l, y, j), col_of(l, y + k, j ^ other_core(l, (y + k) % NY))) for l, y, j in COLS]


L_SWAP = [(col_of(l, y, j), col_of(1 - l, y, j if l == 0 else 1 - j)) for l, y, j in COLS]
CORE_SWAP = [(col_of(l, y, j), col_of(l, y, 1 - j)) for l, y, j in COLS]


def same_core(la, ya, lb, yb):
    dy = lax.rem(yb - ya + NY, NY)
    near = jnp.where(dy == 2, jnp.where(yb >= 2, 1, 0), jnp.where(dy == 3, 0, 1))
    return jnp.where(la != lb, lb, near)


def coordinates():
    r, c = lax.axis_index("row"), lax.axis_index("col")
    return r // NH, r % NH, c // (NY * NC), (c // NC) % NY, c % NC


TN = (((0,), (0,)), ((), ()))
UPPER = [(i, j) for i in range(4) for j in range(i, 4)]


def halves(x):
    high = x.astype(jnp.bfloat16)
    return high, (x - high.astype(jnp.float32)).astype(jnp.bfloat16)


def dot3(a, b):
    ah, al = a
    bh, bl = b

    def dot(x, y):
        return lax.dot_general(x, y, TN, preferred_element_type=jnp.float32)

    return dot(ah, bh) + (dot(ah, bl) + dot(al, bh))


def pick_kernel(a, out, main, other, sems):
    p = main.shape[0]
    z, h, l, y, j = coordinates()
    r = z * NH + h
    take = jnp.where(same_core(r // NY, r % NY, l, y) == 1, j, 1 - j)
    first = pl.multiple_of(take * p, p)
    second = pl.multiple_of((1 - take) * p, p)
    one = pltpu.make_async_copy(a.at[pl.ds(first, p)], main, sems.at[0])
    two = pltpu.make_async_copy(a.at[pl.ds(second, p)], other, sems.at[1])
    one.start()
    two.start()
    one.wait()
    two.wait()
    on_diagonal = r == l * NY + y
    rows = lax.broadcasted_iota(jnp.int32, (p, p), 0)
    cols = lax.broadcasted_iota(jnp.int32, (p, p), 1)

    @pl.when(on_diagonal)
    def _():
        out[0:p] = jnp.where(rows <= cols, main[...], other[...])
        crossing = jnp.sum(jnp.where(rows == cols, other[...], 0.0), axis=0, keepdims=True)
        out[p : p + 8] = jnp.broadcast_to(crossing, (8, p))

    @pl.when(jnp.logical_not(on_diagonal))
    def _():
        out[0:p] = main[...]
        out[p : p + 8] = jnp.zeros((8, p), jnp.float32)


def pick(a):
    p = a.shape[1]
    return pl.pallas_call(
        pick_kernel,
        out_shape=jax.ShapeDtypeStruct((p + 8, p), jnp.float32),
        in_specs=[pl.BlockSpec(memory_space=pl.ANY)],
        out_specs=pl.BlockSpec(memory_space=pltpu.VMEM),
        scratch_shapes=[
            pltpu.VMEM((p, p), jnp.float32),
            pltpu.VMEM((p, p), jnp.float32),
            pltpu.SemaphoreType.DMA((2,)),
        ],
        cost_estimate=pl.CostEstimate(flops=0, bytes_accessed=12 * p * p, transcendentals=0),
        name="pick",
    )(a)


DZ = (0, 3, 1, 2, 0, 3, 1, 2)
DH = (0, 0, 0, 0, 1, 1, 1, 1)


def couple_kernel(pattern, *refs):
    a_in, l_in = refs[0:8], refs[8:17]
    out, a_buf, l_buf, acc, a_sem, l_sem, weight = refs[17:]
    p = acc.shape[0]
    q = p // 4
    z, h, l, y, j = coordinates()
    panel, owner = z * NH + h, l * NY + y
    diagonal = jnp.int32(0)
    for k in range(8):
        pltpu.make_async_copy(a_in[k], a_buf.at[k], a_sem.at[k]).start()
        rk = lax.rem(z + DZ[k], NZ) * NH + (h ^ DH[k])
        la, ya = rk // NY, rk % NY
        dy = lax.rem(ya - y + NY, NY)
        slot = jnp.where(la != l, 4, 0) + jnp.where(dy == 0, 0, jnp.where(dy == 3, 1, jnp.where(dy == 1, 2, 3)))
        for s in range(8):

            @pl.when(slot == s)
            def _():
                pltpu.make_async_copy(l_in[s], l_buf.at[k], l_sem.at[k]).start()

        block = 2 * rk + jnp.where(same_core(la, ya, l, y) == 1, j, 1 - j)
        weight[k] = pattern[block, panel]
        diagonal = jnp.where(rk == owner, k, diagonal)
    weight[8] = pattern[2 * owner + 1 - j, panel]
    weight[9] = pattern[2 * owner + j, panel]
    pltpu.make_async_copy(l_in[8], l_buf.at[8], l_sem.at[8]).start()
    pltpu.make_async_copy(l_in[0], l_buf.at[9], l_sem.at[9]).start()
    acc[...] = jnp.zeros_like(acc)
    rows = lax.broadcasted_iota(jnp.int32, (p, p), 0)
    cols = lax.broadcasted_iota(jnp.int32, (p, p), 1)

    def add(k):
        a = a_buf[k, 0:p] * weight[k].astype(jnp.float32)
        acc[...] += dot3(halves(a), halves(l_buf[k]))

    @pl.loop(0, 8)
    def _(k):
        pltpu.make_async_copy(a_in[0], a_buf.at[k], a_sem.at[k]).wait()
        pltpu.make_async_copy(l_in[0], l_buf.at[k], l_sem.at[k]).wait()

        @pl.when(k == diagonal)
        def _():
            both = a_buf[k, 0:p]
            crossing = a_buf[k, p : p + 1]
            a_buf[8, 0:p] = jnp.where(rows > cols, both, jnp.where(rows == cols, 0.5 * crossing, 0.0))
            a_buf[k, 0:p] = jnp.where(rows < cols, both, jnp.where(rows == cols, 0.5 * both, 0.0))

        add(k)

    pltpu.make_async_copy(l_in[0], l_buf.at[8], l_sem.at[8]).wait()
    add(8)
    pltpu.make_async_copy(l_in[0], l_buf.at[9], l_sem.at[9]).wait()
    half = dot3(halves(l_buf[9] * weight[9].astype(jnp.float32)), halves(acc[...]))
    acc[...] = half
    for n, (i, k) in enumerate(UPPER):
        rows_of, cols_of = slice(i * q, (i + 1) * q), slice(k * q, (k + 1) * q)
        out[pl.ds((n // 2) * q, q), pl.ds((n % 2) * q, q)] = acc[rows_of, cols_of] + acc[cols_of, rows_of].T


def couple(pattern, a_list, l_list):
    p = l_list[0].shape[0]
    anywhere = pl.BlockSpec(memory_space=pl.ANY)
    return pl.pallas_call(
        couple_kernel,
        out_shape=jax.ShapeDtypeStruct((5 * (p // 4), p // 2), jnp.float32),
        in_specs=[pl.BlockSpec(memory_space=pltpu.SMEM)] + [anywhere] * (len(a_list) + len(l_list)),
        out_specs=pl.BlockSpec(memory_space=pltpu.VMEM),
        scratch_shapes=[
            pltpu.VMEM((9, p + 8, p), jnp.float32),
            pltpu.VMEM((10, p, p), jnp.float32),
            pltpu.VMEM((p, p), jnp.float32),
            pltpu.SemaphoreType.DMA((8,)),
            pltpu.SemaphoreType.DMA((10,)),
            pltpu.SMEM((10,), jnp.int32),
        ],
        compiler_params=pltpu.CompilerParams(vmem_limit_bytes=40 << 20),
        cost_estimate=pl.CostEstimate(flops=60 * p**3, bytes_accessed=19 * p * p * 4, transcendentals=0),
        name="couple",
    )(pattern, *a_list, *l_list)


def thirds(x):
    high = x.astype(jnp.bfloat16)
    rest = x - high.astype(jnp.float32)
    middle = rest.astype(jnp.bfloat16)
    return high, middle, (rest - middle.astype(jnp.float32)).astype(jnp.bfloat16)


def indicator(mask):
    return jnp.where(mask, 1.0, 0.0)


def nn(x, y):
    return jnp.dot(x, y, preferred_element_type=jnp.float32)


def slot_kernel(panels, values, slotted, places):
    items = panels.shape[1]
    slots = slotted.shape[0]
    n_panels = 8
    capacity = slots // n_panels
    before = indicator(
        lax.broadcasted_iota(jnp.int32, (items, items), 0) < lax.broadcasted_iota(jnp.int32, (items, items), 1)
    ).astype(jnp.bfloat16)
    panel_of = lax.broadcasted_iota(jnp.int32, (n_panels, items), 0)
    slot_of = lax.broadcasted_iota(jnp.int32, (slots, items), 0)
    base = jnp.zeros((n_panels, 1), jnp.float32)
    total = None
    for k in range(2):
        panel = panels[k : k + 1, :]
        member = indicator(panel_of == panel)
        rank = nn(member.astype(jnp.bfloat16), before) + base
        base = base + jnp.sum(member, axis=1, keepdims=True)
        place = jnp.sum(member * rank, axis=0, keepdims=True).astype(jnp.int32)
        places[k : k + 1, :] = place
        chosen = indicator(slot_of == panel * capacity + place).astype(jnp.bfloat16)
        for piece in thirds(values[:, k, :]):
            part = nn(chosen, piece)
            total = part if total is None else total + part
    slotted[...] = total


def slot_entries(panels, values, capacity):
    items, _, p = values.shape
    return pl.pallas_call(
        slot_kernel,
        out_shape=(
            jax.ShapeDtypeStruct((8 * capacity, p), jnp.float32),
            jax.ShapeDtypeStruct((2, items), jnp.int32),
        ),
        in_specs=[pl.BlockSpec(memory_space=pltpu.VMEM)] * 2,
        out_specs=(pl.BlockSpec(memory_space=pltpu.VMEM),) * 2,
        cost_estimate=pl.CostEstimate(flops=12 * capacity * 8 * items * p, bytes_accessed=12 * items * p * 4, transcendentals=0),
        name="slot_entries",
    )(panels, values)


def forms_kernel(packed, d, x, out, forms):
    p = d.shape[0]
    q = p // 4
    capacity = forms.shape[1]
    step = 4 * capacity
    for n, (i, j) in enumerate(UPPER):
        rows, cols = slice(i * q, (i + 1) * q), slice(j * q, (j + 1) * q)
        block = packed[pl.ds((n // 2) * q, q), pl.ds((n % 2) * q, q)]
        out[rows, cols] = d[rows, cols] + block
        if i != j:
            out[cols, rows] = d[cols, rows] + block.T
    high, low = halves(out[...])
    for first in range(2):
        here = x[first * step : (first + 1) * step, :]
        x_high, x_low = halves(here)
        terms = (nn(x_high, high) + (nn(x_high, low) + nn(x_low, high))) * here
        lanes = terms[:, 0:q] + terms[:, q : 2 * q] + (terms[:, 2 * q : 3 * q] + terms[:, 3 * q :])
        for panel in range(4):
            mine = lanes[panel * capacity : (panel + 1) * capacity, :]
            forms[pl.ds(first * 4 + panel, 1), :] = jnp.sum(mine.T, axis=0, keepdims=True)


def forms_of(packed, d, x, capacity):
    p = d.shape[0]
    return pl.pallas_call(
        forms_kernel,
        out_shape=(
            jax.ShapeDtypeStruct(d.shape, jnp.float32),
            jax.ShapeDtypeStruct((8, capacity), jnp.float32),
        ),
        in_specs=[pl.BlockSpec(memory_space=pltpu.VMEM)] * 3,
        out_specs=(pl.BlockSpec(memory_space=pltpu.VMEM),) * 2,
        cost_estimate=pl.CostEstimate(flops=48 * capacity * p * p, bytes_accessed=20 * p * p, transcendentals=0),
        name="forms",
    )(packed, d, x)


def finish_kernel(panels, places, answers, out):
    n_panels, capacity = answers.shape
    items = panels.shape[1]
    panel_of = lax.broadcasted_iota(jnp.int32, (n_panels, items), 0)
    place_of = lax.broadcasted_iota(jnp.int32, (capacity, items), 0)
    pieces = thirds(answers[...])
    total = jnp.zeros((1, items), jnp.float32)
    for k in range(2):
        chosen = indicator(place_of == places[k : k + 1, :]).astype(jnp.bfloat16)
        columns = nn(pieces[0], chosen) + nn(pieces[1], chosen) + nn(pieces[2], chosen)
        member = panel_of == panels[k : k + 1, :]
        total += jnp.sum(jnp.where(member, columns, 0.0), axis=0, keepdims=True)
    out[...] = total


def finish(panels, places, answers):
    return pl.pallas_call(
        finish_kernel,
        out_shape=jax.ShapeDtypeStruct((1, panels.shape[1]), jnp.float32),
        in_specs=[pl.BlockSpec(memory_space=pltpu.VMEM)] * 3,
        out_specs=pl.BlockSpec(memory_space=pltpu.VMEM),
        name="finish",
    )(panels, places, answers)


def exchange(x, axis):
    return lax.all_to_all(x, axis, split_axis=0, concat_axis=0, tiled=True)


def body(inverse_anc, factor, pattern, d_inverse, jac_blocks, jac_values):
    p = factor.shape[0]
    n_row = lax.axis_size("row")
    n_col = lax.axis_size("col")

    panels = jac_blocks.T
    capacity = 2 * jac_values.shape[0] * jac_values.shape[1] // n_row

    def keep(lb, yb):
        return 0

    def turn(lb, yb):
        return 1

    def turn_low(lb, yb):
        return 0 if yb >= 2 else 1

    l0 = factor
    l1 = lax.ppermute(l0, "col", L_SWAP)
    l0m = lax.ppermute(l0, "col", y_shift(1, keep))
    l0p = lax.ppermute(l0, "col", y_shift(-1, turn))
    a0 = pick(inverse_anc)
    a0m = lax.ppermute(a0, "row", z_shift(1))
    a0p = lax.ppermute(a0, "row", z_shift(-1))
    l_core = lax.ppermute(l0, "col", CORE_SWAP)
    a1 = lax.ppermute(a0, "row", H_SWAP)
    l1m = lax.ppermute(l1, "col", y_shift(1, keep))
    l1p = lax.ppermute(l1, "col", y_shift(-1, keep))
    a0f = lax.ppermute(a0m, "row", z_shift(1))
    l0f = lax.ppermute(l0m, "col", y_shift(1, turn_low))
    a1m = lax.ppermute(a1, "row", z_shift(1))
    a1p = lax.ppermute(a1, "row", z_shift(-1))
    l1f = lax.ppermute(l1p, "col", y_shift(-1, keep))
    a1f = lax.ppermute(a0f, "row", H_SWAP)
    slotted, places = slot_entries(panels, jac_values, capacity)
    slots_in = exchange(slotted.reshape(n_row, capacity, p), "row")
    partial_value = couple(
        pattern,
        [a0, a0m, a0p, a0f, a1, a1m, a1p, a1f],
        [l0, l0m, l0p, l0f, l1, l1m, l1p, l1f, l_core],
    )
    pieces = partial_value.reshape(n_col, -1, p // 2)
    pieces = exchange(pieces, "col")
    own = jnp.sum(pieces, axis=0)
    whole = exchange(jnp.broadcast_to(own[None], pieces.shape), "col")
    diag_block, forms = forms_of(whole.reshape(partial_value.shape), d_inverse, slots_in.reshape(-1, p), capacity)
    answers = exchange(forms, "row")
    variance = finish(panels, places, answers).reshape(-1)
    return (diag_block, variance)


def solution(mesh):
    return jax.shard_map(
        body,
        mesh=mesh,
        in_specs=(
            P("row", "col"),
            P("col", "row"),
            P(),
            P("row", None),
            P(("row", "col"), None),
            P(("row", "col"), None, None),
        ),
        out_specs=(P("row", None), P(("row", "col"))),
        check_vma=False,
    )
```

profile of v0, /device:TPU:24, one launch (start us, length us, event | category | flops | bytes accessed | tf_op | source)
XLA Modules:
  0.0 193.5 jit_solution(16143097963020196262)
XLA Ops:
  0.6 2.7 %pick.1.refs_0_ = f32[520,512]{1,0:T(8,128)} custom-call(f32[1024,512]{1,0:T(8,128)} %a.1), custom_call_target="tpu_custom_call" | custom-call | bytes 3145728 | tf_op jit(solution)/shard_map/pick/pallas_call | solution.py:97
  3.4 2.0 %collective-permute-start = (f32[520,512]{1,0:T(8,128)}, f32[520,512]{1,0:T(8,128)S(1)}, u32[]{:S(2)}, u32[]{:S(2)}) collective-permute-start(f32[520,512]{1,0:T(8,128)} %pick.1.refs_0_), channel_id=1, source_target_pairs={{0,32},{16,48},{32,64},{48,80},{64,96},{80,112},{96,0},{112,16},{1... | collective-permute-start | bytes 3194888 | tf_op jit(solution)/shard_map/ppermute | solution.py:341
  5.3 1.5 collective-permute-start.10
  6.8 2.1 %collective-permute-start.7 = (f32[512,512]{1,0:T(8,128)}, f32[512,512]{1,0:T(8,128)}, u32[]{:S(2)}, u32[]{:S(2)}) collective-permute-start(f32[512,512]{1,0:T(8,128)} %refs_8_.1), channel_id=1, source_target_pairs={{0,2},{1,3},{2,4},{3,5},{4,6},{5,7},{6,0},{7,1},{8,10},{9,11},{10,... | collective-permute-start | bytes 3145736 | tf_op jit(solution)/shard_map/ppermute | solution.py:338
  9.9 21.1 %collective-permute-done.10.refs_12_ = f32[512,512]{1,0:T(8,128)S(1)} collective-permute-done((f32[512,512]{1,0:T(8,128)}, f32[512,512]{1,0:T(8,128)S(1)}, u32[]{:S(2)}, u32[]{:S(2)}) %collective-permute-start.10) | collective-permute-done | bytes 1048608 | tf_op jit(solution)/shard_map/ppermute | solution.py:337
  31.0 2.8 %collective-permute-start.3 = (f32[520,512]{1,0:T(8,128)}, f32[520,512]{1,0:T(8,128)}, u32[]{:S(2)}, u32[]{:S(2)}) collective-permute-start(f32[520,512]{1,0:T(8,128)} %pick.1.refs_0_), channel_id=1, source_target_pairs={{0,16},{16,0},{32,48},{48,32},{64,80},{80,64},{96,112},{112,96},{1... | collective-permute-start | bytes 3194888 | tf_op jit(solution)/shard_map/ppermute | solution.py:344
  34.8 2.4 %collective-permute-start.1 = (f32[520,512]{1,0:T(8,128)}, f32[520,512]{1,0:T(8,128)S(1)}, u32[]{:S(2)}, u32[]{:S(2)}) collective-permute-start(f32[520,512]{1,0:T(8,128)} %pick.1.refs_0_), channel_id=1, source_target_pairs={{0,96},{16,112},{32,0},{48,16},{64,32},{80,48},{96,64},{112,80},{1... | collective-permute-start | bytes 3194888 | tf_op jit(solution)/shard_map/ppermute | solution.py:342
  39.0 2.5 %collective-permute-start.11 = (f32[512,512]{1,0:T(8,128)S(1)}, f32[512,512]{1,0:T(8,128)S(1)}, u32[]{:S(2)}, u32[]{:S(2)}) collective-permute-start(f32[512,512]{1,0:T(8,128)S(1)} %collective-permute-done.10.refs_12_), channel_id=1, source_target_pairs={{0,2},{1,3},{2,4},{3,5},{4,6},{5,7},{6,0},{7,1},{8,10},{9,11},{10,... | collective-permute-start | bytes 3145736 | tf_op jit(solution)/shard_map/ppermute | solution.py:345
  42.5 16.0 %collective-permute-done.3.refs_4_ = f32[520,512]{1,0:T(8,128)} collective-permute-done((f32[520,512]{1,0:T(8,128)}, f32[520,512]{1,0:T(8,128)}, u32[]{:S(2)}, u32[]{:S(2)}) %collective-permute-start.3) | collective-permute-done | bytes 1064992 | tf_op jit(solution)/shard_map/ppermute | solution.py:344
  58.5 2.2 %collective-permute-start.5 = (f32[520,512]{1,0:T(8,128)}, f32[520,512]{1,0:T(8,128)}, u32[]{:S(2)}, u32[]{:S(2)}) collective-permute-start(f32[520,512]{1,0:T(8,128)} %collective-permute-done.3.refs_4_), channel_id=1, source_target_pairs={{0,96},{16,112},{32,0},{48,16},{64,32},{80,48},{96,64},{112,80},{1... | collective-permute-start | bytes 3194888 | tf_op jit(solution)/shard_map/ppermute | solution.py:350
  62.0 1.5 collective-permute-done.2.refs_3_
  63.5 2.1 %collective-permute-start.6 = (f32[520,512]{1,0:T(8,128)S(1)}, f32[520,512]{1,0:T(8,128)}, u32[]{:S(2)}, u32[]{:S(2)}) collective-permute-start(f32[520,512]{1,0:T(8,128)S(1)} %collective-permute-done.2.refs_3_), channel_id=1, source_target_pairs={{0,16},{16,0},{32,48},{48,32},{64,80},{80,64},{96,112},{112,96},{1... | collective-permute-start | bytes 3194888 | tf_op jit(solution)/shard_map/ppermute | solution.py:352
  66.6 2.0 %collective-permute-start.13 = (f32[512,512]{1,0:T(8,128)}, f32[512,512]{1,0:T(8,128)}, u32[]{:S(2)}, u32[]{:S(2)}) collective-permute-start(f32[512,512]{1,0:T(8,128)} %collective-permute-done.12.refs_14_), channel_id=1, source_target_pairs={{0,6},{1,7},{2,0},{3,1},{4,2},{5,3},{6,4},{7,5},{8,14},{9,15},{10,... | collective-permute-start | bytes 3145736 | tf_op jit(solution)/shard_map/ppermute | solution.py:351
  68.7 20.8 %collective-permute-done.9.refs_11_ = f32[512,512]{1,0:T(8,128)} collective-permute-done((f32[512,512]{1,0:T(8,128)}, f32[512,512]{1,0:T(8,128)}, u32[]{:S(2)}, u32[]{:S(2)}) %collective-permute-start.9) | collective-permute-done | bytes 1048608 | tf_op jit(solution)/shard_map/ppermute | solution.py:348
  89.5 3.7 %collective-permute-done.13.refs_15_ = f32[512,512]{1,0:T(8,128)} collective-permute-done((f32[512,512]{1,0:T(8,128)}, f32[512,512]{1,0:T(8,128)}, u32[]{:S(2)}, u32[]{:S(2)}) %collective-permute-start.13) | collective-permute-done | bytes 1048608 | tf_op jit(solution)/shard_map/ppermute | solution.py:351
  99.4 13.6 %couple.1 = f32[640,256]{1,0:T(8,128)} custom-call(s32[16,8]{1,0:T(8,128)S(1)} %copy.9.pattern, f32[520,512]{1,0:T(8,128)S(1)} %copy-done, f32[520,512]{1,0:T(8,128)S(1)} %collective-permute-done.refs_1_, f32[520,512]{1,0:T(8,128)S(1)} %collective-permute-done.1.refs_2_, f32[520,512]{1,0:T(8,128)S(1)} %collective-permute-done.2.refs_3_, ...), custom_call_target="tpu_custom_call" | custom-call | flops 8053063680 | bytes 19922944 | tf_op jit(solution)/shard_map/couple/pallas_call | solution.py:178
  113.0 4.5 %all-to-all-start = ((f32[16,40,256]{2,1,0:T(8,128)}), f32[16,40,256]{2,1,0:T(8,128)S(1)}, u32[]{:S(2)}, u32[]{:S(2)}) async-start(f32[16,40,256]{2,1,0:T(8,128)} %bitcast), calls=%async_computation | async-start | bytes 1310720 | tf_op jit(solution)/shard_map/all_to_all | solution.py:316
  117.5 9.2 %slot_entries.1 = (f32[1024,512]{1,0:T(8,128)}, s32[2,256]{1,0:T(2,128)}) custom-call(s32[2,256]{1,0:T(2,128)} %bitcast.15, f32[256,2,512]{2,1,0:T(2,128)} %values.1), custom_call_target="tpu_custom_call" | custom-call | flops 1610612736 | bytes 6291456 | tf_op jit(solution)/shard_map/slot_entries/pallas_call | solution.py:240
  127.5 4.7 %all-to-all-start.2 = ((f32[8,128,512]{2,1,0:T(8,128)}), f32[8,128,512]{2,1,0:T(8,128)S(1)}, u32[]{:S(2)}, u32[]{:S(2)}) async-start(f32[8,128,512]{2,1,0:T(8,128)} %bitcast.11), calls=%async_computation.2 | async-start | bytes 4194304 | tf_op jit(solution)/shard_map/all_to_all | solution.py:316
  132.3 28.9 %all-to-all-done.2 = f32[8,128,512]{2,1,0:T(8,128)S(1)} async-done(((f32[8,128,512]{2,1,0:T(8,128)}), f32[8,128,512]{2,1,0:T(8,128)S(1)}, u32[]{:S(2)}, u32[]{:S(2)}) %all-to-all-start.2) | async-done | bytes 2097184 | tf_op jit(solution)/shard_map/all_to_all | solution.py:316
  161.2 14.6 %all_to_all.26 = f32[16,40,256]{2,1,0:T(8,128)} all-to-all(f32[16,40,256]{2,1,0:T(8,128)S(1)} %broadcast_in_dim.2), channel_id=1, replica_groups=mesh['row'=8,'col'=16] {'col'}, dimensions={0} | all-to-all | bytes 1310720 | tf_op jit(solution)/shard_map/all_to_all | solution.py:316
  175.9 4.6 %forms.1 = (f32[512,512]{1,0:T(8,128)}, f32[8,128]{1,0:T(8,128)}) custom-call(f32[640,256]{1,0:T(8,128)} %bitcast.12, f32[512,512]{1,0:T(8,128)} %d.1, f32[1024,512]{1,0:T(8,128)} %bitcast.10), custom_call_target="tpu_custom_call" | custom-call | flops 1610612736 | bytes 5242880 | tf_op jit(solution)/shard_map/forms/pallas_call | solution.py:277
  180.5 11.6 %all_to_all.27 = f32[8,1,128]{2,1,0:T(1,128)} all-to-all(f32[8,1,128]{2,1,0:T(1,128)} %bitcast.14), channel_id=1, replica_groups=mesh['row'=8,'col'=16] {'row'}, dimensions={0} | all-to-all | bytes 8192 | tf_op jit(solution)/shard_map/all_to_all | solution.py:316
  192.1 1.4 finish.1
  (42 shorter events, 14.2 us)
Async XLA Ops:
  0.6 68.0 %copy-start.10 = (s32[16,8]{0,1:T(8,128)S(1)}, s32[16,8]{0,1:T(8,128)}, u32[]{:S(2)}) copy-start(s32[16,8]{0,1:T(8,128)} %param.8) | copy-start | bytes 1540
  3.4 33.8 %collective-permute-start = (f32[520,512]{1,0:T(8,128)}, f32[520,512]{1,0:T(8,128)S(1)}, u32[]{:S(2)}, u32[]{:S(2)}) collective-permute-start(f32[520,512]{1,0:T(8,128)} %pick.1.refs_0_), channel_id=1, source_target_pairs={{0,32},{16,48},{32,64},{48,80},{64,96},{80,112},{96,0},{112,16},{1... | collective-permute-start | bytes 3194888 | tf_op jit(solution)/shard_map/ppermute | solution.py:341
  5.3 25.6 %collective-permute-start.10 = (f32[512,512]{1,0:T(8,128)}, f32[512,512]{1,0:T(8,128)S(1)}, u32[]{:S(2)}, u32[]{:S(2)}) collective-permute-start(f32[512,512]{1,0:T(8,128)} %refs_8_.1), channel_id=1, source_target_pairs={{0,8},{1,9},{2,10},{3,11},{4,12},{5,13},{6,14},{7,15},{8,1},{9,0},... | collective-permute-start | bytes 3145736 | tf_op jit(solution)/shard_map/ppermute | solution.py:337
  6.8 27.0 %collective-permute-start.8 = (f32[512,512]{1,0:T(8,128)}, f32[512,512]{1,0:T(8,128)S(1)}, u32[]{:S(2)}, u32[]{:S(2)}) collective-permute-start(f32[512,512]{1,0:T(8,128)} %refs_8_.1), channel_id=1, source_target_pairs={{0,7},{1,6},{2,1},{3,0},{4,3},{5,2},{6,5},{7,4},{8,15},{9,14},{10,... | collective-permute-start | bytes 3145736 | tf_op jit(solution)/shard_map/ppermute | solution.py:339
  6.8 30.4 %collective-permute-start.7 = (f32[512,512]{1,0:T(8,128)}, f32[512,512]{1,0:T(8,128)}, u32[]{:S(2)}, u32[]{:S(2)}) collective-permute-start(f32[512,512]{1,0:T(8,128)} %refs_8_.1), channel_id=1, source_target_pairs={{0,2},{1,3},{2,4},{3,5},{4,6},{5,7},{6,0},{7,1},{8,10},{9,11},{10,... | collective-permute-start | bytes 3145736 | tf_op jit(solution)/shard_map/ppermute | solution.py:338
  9.0 29.1 %collective-permute-start.14 = (f32[512,512]{1,0:T(8,128)}, f32[512,512]{1,0:T(8,128)S(1)}, u32[]{:S(2)}, u32[]{:S(2)}) collective-permute-start(f32[512,512]{1,0:T(8,128)} %refs_8_.1), channel_id=1, source_target_pairs={{0,1},{1,0},{2,3},{3,2},{4,5},{5,4},{6,7},{7,6},{8,9},{9,8},{10,11... | collective-permute-start | bytes 3145736 | tf_op jit(solution)/shard_map/ppermute | solution.py:343
  31.0 27.5 %collective-permute-start.3 = (f32[520,512]{1,0:T(8,128)}, f32[520,512]{1,0:T(8,128)}, u32[]{:S(2)}, u32[]{:S(2)}) collective-permute-start(f32[520,512]{1,0:T(8,128)} %pick.1.refs_0_), channel_id=1, source_target_pairs={{0,16},{16,0},{32,48},{48,32},{64,80},{80,64},{96,112},{112,96},{1... | collective-permute-start | bytes 3194888 | tf_op jit(solution)/shard_map/ppermute | solution.py:344
  34.8 25.9 %collective-permute-start.1 = (f32[520,512]{1,0:T(8,128)}, f32[520,512]{1,0:T(8,128)S(1)}, u32[]{:S(2)}, u32[]{:S(2)}) collective-permute-start(f32[520,512]{1,0:T(8,128)} %pick.1.refs_0_), channel_id=1, source_target_pairs={{0,96},{16,112},{32,0},{48,16},{64,32},{80,48},{96,64},{112,80},{1... | collective-permute-start | bytes 3194888 | tf_op jit(solution)/shard_map/ppermute | solution.py:342
  37.2 26.3 %collective-permute-start.2 = (f32[520,512]{1,0:T(8,128)S(1)}, f32[520,512]{1,0:T(8,128)S(1)}, u32[]{:S(2)}, u32[]{:S(2)}) collective-permute-start(f32[520,512]{1,0:T(8,128)S(1)} %collective-permute-done.refs_1_), channel_id=1, source_target_pairs={{0,32},{16,48},{32,64},{48,80},{64,96},{80,112},{96,0},{112,16},{1... | collective-permute-start | bytes 3194888 | tf_op jit(solution)/shard_map/ppermute | solution.py:347
  37.2 28.4 %collective-permute-start.12 = (f32[512,512]{1,0:T(8,128)S(1)}, f32[512,512]{1,0:T(8,128)}, u32[]{:S(2)}, u32[]{:S(2)}) collective-permute-start(f32[512,512]{1,0:T(8,128)S(1)} %collective-permute-done.10.refs_12_), channel_id=1, source_target_pairs={{0,6},{1,7},{2,0},{3,1},{4,2},{5,3},{6,4},{7,5},{8,14},{9,15},{10,... | collective-permute-start | bytes 3145736 | tf_op jit(solution)/shard_map/ppermute | solution.py:346
  39.0 26.6 %collective-permute-start.11 = (f32[512,512]{1,0:T(8,128)S(1)}, f32[512,512]{1,0:T(8,128)S(1)}, u32[]{:S(2)}, u32[]{:S(2)}) collective-permute-start(f32[512,512]{1,0:T(8,128)S(1)} %collective-permute-done.10.refs_12_), channel_id=1, source_target_pairs={{0,2},{1,3},{2,4},{3,5},{4,6},{5,7},{6,0},{7,1},{8,10},{9,11},{10,... | collective-permute-start | bytes 3145736 | tf_op jit(solution)/shard_map/ppermute | solution.py:345
  58.5 31.0 %collective-permute-start.5 = (f32[520,512]{1,0:T(8,128)}, f32[520,512]{1,0:T(8,128)}, u32[]{:S(2)}, u32[]{:S(2)}) collective-permute-start(f32[520,512]{1,0:T(8,128)} %collective-permute-done.3.refs_4_), channel_id=1, source_target_pairs={{0,96},{16,112},{32,0},{48,16},{64,32},{80,48},{96,64},{112,80},{1... | collective-permute-start | bytes 3194888 | tf_op jit(solution)/shard_map/ppermute | solution.py:350
  60.7 28.8 %collective-permute-start.4 = (f32[520,512]{1,0:T(8,128)}, f32[520,512]{1,0:T(8,128)}, u32[]{:S(2)}, u32[]{:S(2)}) collective-permute-start(f32[520,512]{1,0:T(8,128)} %collective-permute-done.3.refs_4_), channel_id=1, source_target_pairs={{0,32},{16,48},{32,64},{48,80},{64,96},{80,112},{96,0},{112,16},{1... | collective-permute-start | bytes 3194888 | tf_op jit(solution)/shard_map/ppermute | solution.py:349
  63.5 29.7 %collective-permute-start.6 = (f32[520,512]{1,0:T(8,128)S(1)}, f32[520,512]{1,0:T(8,128)}, u32[]{:S(2)}, u32[]{:S(2)}) collective-permute-start(f32[520,512]{1,0:T(8,128)S(1)} %collective-permute-done.2.refs_3_), channel_id=1, source_target_pairs={{0,16},{16,0},{32,48},{48,32},{64,80},{80,64},{96,112},{112,96},{1... | collective-permute-start | bytes 3194888 | tf_op jit(solution)/shard_map/ppermute | solution.py:352
  65.6 23.9 %collective-permute-start.9 = (f32[512,512]{1,0:T(8,128)}, f32[512,512]{1,0:T(8,128)}, u32[]{:S(2)}, u32[]{:S(2)}) collective-permute-start(f32[512,512]{1,0:T(8,128)} %collective-permute-done.7.refs_9_), channel_id=1, source_target_pairs={{0,3},{1,2},{2,4},{3,5},{4,6},{5,7},{6,1},{7,0},{8,11},{9,10},{10,... | collective-permute-start | bytes 3145736 | tf_op jit(solution)/shard_map/ppermute | solution.py:348
  66.6 26.6 %collective-permute-start.13 = (f32[512,512]{1,0:T(8,128)}, f32[512,512]{1,0:T(8,128)}, u32[]{:S(2)}, u32[]{:S(2)}) collective-permute-start(f32[512,512]{1,0:T(8,128)} %collective-permute-done.12.refs_14_), channel_id=1, source_target_pairs={{0,6},{1,7},{2,0},{3,1},{4,2},{5,3},{6,4},{7,5},{8,14},{9,15},{10,... | collective-permute-start | bytes 3145736 | tf_op jit(solution)/shard_map/ppermute | solution.py:351
  93.2 1.2 copy-start
  94.5 1.2 copy-start.2
  95.7 1.2 copy-start.4
  96.9 1.2 copy-start.6
  98.1 1.2 copy-start.8
  113.0 14.6 %all-to-all-start = ((f32[16,40,256]{2,1,0:T(8,128)}), f32[16,40,256]{2,1,0:T(8,128)S(1)}, u32[]{:S(2)}, u32[]{:S(2)}) async-start(f32[16,40,256]{2,1,0:T(8,128)} %bitcast), calls=%async_computation | async-start | bytes 1310720 | tf_op jit(solution)/shard_map/all_to_all | solution.py:316
  127.5 33.6 %all-to-all-start.2 = ((f32[8,128,512]{2,1,0:T(8,128)}), f32[8,128,512]{2,1,0:T(8,128)S(1)}, u32[]{:S(2)}, u32[]{:S(2)}) async-start(f32[8,128,512]{2,1,0:T(8,128)} %bitcast.11), calls=%async_computation.2 | async-start | bytes 4194304 | tf_op jit(solution)/shard_map/all_to_all | solution.py:316
  161.2 14.7 %copy-start.9 = (f32[8,128,512]{2,1,0:T(8,128)}, f32[8,128,512]{2,1,0:T(8,128)S(1)}, u32[]{:S(2)}) copy-start(f32[8,128,512]{2,1,0:T(8,128)S(1)} %all-to-all-done.2) | copy-start | bytes 6291460
  (4 other events, 3.9 us)
where the time goes:
time: 196 us; the launch traced here: 194 us
  waiting for transfers between devices  92.8 us (47%)
  starting transfers between devices  31.9 us (16%)
  Pallas kernels  31.6 us (16%)
  blocking collectives  26.2 us (13%)
  local copies, waits for them, and re-layouts  10.2 us (5%)
    all_to_all x2, waiting for transfers between devices, exchange(): return lax.all_to_all(x, axis, split_axis=0, concat_axis=0, tiled=True)  29.7 us
    all_to_all x2, blocking collectives, exchange(): return lax.all_to_all(x, axis, split_axis=0, concat_axis=0, tiled=True)  26.2 us
    ppermute x1, waiting for transfers between devices, body(): l1 = lax.ppermute(l0, 'col', L_SWAP)  21.1 us
    ppermute x1, waiting for transfers between devices, body(): l0f = lax.ppermute(l0m, 'col', y_shift(1, turn_low))  20.8 us
    ppermute x1, waiting for transfers between devices, body(): a1 = lax.ppermute(a0, 'row', H_SWAP)  16 us
    pallas_call x1, Pallas kernels, couple(): pl.pallas_call(couple_kernel, out_shape=jax.ShapeDtypeStruct((5 * (p // 4...  13.6 us
    unnamed x23, local copies, waits for them, and re-layouts  10.1 us
    pallas_call x1, Pallas kernels, slot_entries(): pl.pallas_call(slot_kernel, out_shape=(jax.ShapeDtypeStruct((8 * capacity...  9.22 us
  transfers between devices with their start and end apart: 17, of which 7 were waited for; matrix products, arithmetic and copies ran while one was open for 0% of the time, Pallas kernels for 5%

commit v1 on v0

--- a/solution.py
+++ b/solution.py
@@ -111,87 +111,146 @@
 
 DZ = (0, 3, 1, 2, 0, 3, 1, 2)
 DH = (0, 0, 0, 0, 1, 1, 1, 1)
-
-
-def couple_kernel(pattern, *refs):
-    a_in, l_in = refs[0:8], refs[8:17]
-    out, a_buf, l_buf, acc, a_sem, l_sem, weight = refs[17:]
+EARLY_A = (0, 1, 2, 3, 4)
+EARLY_L = (0, 1, 2, 4, 5, 6, 8)
+
+
+def add_products(early, pattern, a_in, l_in, a_buf, l_buf, acc, a_sem, l_sem, weight):
     p = acc.shape[0]
-    q = p // 4
     z, h, l, y, j = coordinates()
     panel, owner = z * NH + h, l * NY + y
-    diagonal = jnp.int32(0)
+    diagonal = jnp.int32(-1)
     for k in range(8):
-        pltpu.make_async_copy(a_in[k], a_buf.at[k], a_sem.at[k]).start()
         rk = lax.rem(z + DZ[k], NZ) * NH + (h ^ DH[k])
         la, ya = rk // NY, rk % NY
         dy = lax.rem(ya - y + NY, NY)
         slot = jnp.where(la != l, 4, 0) + jnp.where(dy == 0, 0, jnp.where(dy == 3, 1, jnp.where(dy == 1, 2, 3)))
-        for s in range(8):
-
-            @pl.when(slot == s)
+        ready = jnp.where(dy == 2, 0, 1) if k in EARLY_A else jnp.int32(0)
+        active = ready == 1 if early else ready == 0
+        if k in a_in:
+
+            @pl.when(active)
             def _():
-                pltpu.make_async_copy(l_in[s], l_buf.at[k], l_sem.at[k]).start()
+                pltpu.make_async_copy(a_in[k], a_buf.at[k], a_sem.at[k]).start()
+
+            for s in range(8):
+                if s in l_in:
+
+                    @pl.when(jnp.logical_and(active, slot == s))
+                    def _():
+                        pltpu.make_async_copy(l_in[s], l_buf.at[k], l_sem.at[k]).start()
 
         block = 2 * rk + jnp.where(same_core(la, ya, l, y) == 1, j, 1 - j)
         weight[k] = pattern[block, panel]
-        diagonal = jnp.where(rk == owner, k, diagonal)
-    weight[8] = pattern[2 * owner + 1 - j, panel]
-    weight[9] = pattern[2 * owner + j, panel]
-    pltpu.make_async_copy(l_in[8], l_buf.at[8], l_sem.at[8]).start()
-    pltpu.make_async_copy(l_in[0], l_buf.at[9], l_sem.at[9]).start()
+        weight[k + 8] = jnp.where(active, 1, 0)
+        diagonal = jnp.where(jnp.logical_and(rk == owner, active), k, diagonal)
+
+    @pl.when(diagonal >= 0)
+    def _():
+        pltpu.make_async_copy(l_in[8], l_buf.at[8], l_sem.at[8]).start()
+
     acc[...] = jnp.zeros_like(acc)
     rows = lax.broadcasted_iota(jnp.int32, (p, p), 0)
     cols = lax.broadcasted_iota(jnp.int32, (p, p), 1)
 
-    def add(k):
-        a = a_buf[k, 0:p] * weight[k].astype(jnp.float32)
-        acc[...] += dot3(halves(a), halves(l_buf[k]))
-
-    @pl.loop(0, 8)
+    @pl.loop(0, 9)
     def _(k):
-        pltpu.make_async_copy(a_in[0], a_buf.at[k], a_sem.at[k]).wait()
-        pltpu.make_async_copy(l_in[0], l_buf.at[k], l_sem.at[k]).wait()
-
-        @pl.when(k == diagonal)
+        usual = jnp.minimum(k, 7)
+        spare = jnp.logical_and(k == 8, diagonal >= 0)
+        active = jnp.logical_or(jnp.logical_and(k < 8, weight[usual + 8] == 1), spare)
+
+        @pl.when(active)
         def _():
-            both = a_buf[k, 0:p]
-            crossing = a_buf[k, p : p + 1]
-            a_buf[8, 0:p] = jnp.where(rows > cols, both, jnp.where(rows == cols, 0.5 * crossing, 0.0))
-            a_buf[k, 0:p] = jnp.where(rows < cols, both, jnp.where(rows == cols, 0.5 * both, 0.0))
-
-        add(k)
-
-    pltpu.make_async_copy(l_in[0], l_buf.at[8], l_sem.at[8]).wait()
-    add(8)
-    pltpu.make_async_copy(l_in[0], l_buf.at[9], l_sem.at[9]).wait()
-    half = dot3(halves(l_buf[9] * weight[9].astype(jnp.float32)), halves(acc[...]))
+            @pl.when(k < 8)
+            def _():
+                pltpu.make_async_copy(a_in[0], a_buf.at[usual], a_sem.at[usual]).wait()
+
+            pltpu.make_async_copy(l_in[0], l_buf.at[k], l_sem.at[k]).wait()
+
+            @pl.when(k == diagonal)
+            def _():
+                both = a_buf[k, 0:p]
+                crossing = a_buf[k, p : p + 1]
+                a_buf[8, 0:p] = jnp.where(rows > cols, both, jnp.where(rows == cols, 0.5 * crossing, 0.0))
+                a_buf[k, 0:p] = jnp.where(rows < cols, both, jnp.where(rows == cols, 0.5 * both, 0.0))
+
+            factor = jnp.where(k == 8, pattern[2 * owner + 1 - j, panel], weight[usual])
+            a = a_buf[k, 0:p] * factor.astype(jnp.float32)
+            acc[...] += dot3(halves(a), halves(l_buf[k]))
+
+
+def early_kernel(pattern, *refs):
+    count = len(EARLY_A) + len(EARLY_L)
+    a_in = dict(zip(EARLY_A, refs[: len(EARLY_A)]))
+    l_in = dict(zip(EARLY_L, refs[len(EARLY_A) : count]))
+    acc, a_buf, l_buf, a_sem, l_sem, weight = refs[count:]
+    add_products(True, pattern, a_in, l_in, a_buf, l_buf, acc, a_sem, l_sem, weight)
+
+
+def late_kernel(pattern, before, *refs):
+    a_in = dict(enumerate(refs[0:8]))
+    l_in = dict(enumerate(refs[8:17]))
+    out, a_buf, l_buf, acc, sums, a_sem, l_sem, more_sem, weight = refs[17:]
+    p = acc.shape[0]
+    q = p // 4
+    z, h, l, y, j = coordinates()
+    own = pltpu.make_async_copy(l_in[0], l_buf.at[9], more_sem.at[0])
+    sofar = pltpu.make_async_copy(before, sums, more_sem.at[1])
+    own.start()
+    sofar.start()
+    add_products(False, pattern, a_in, l_in, a_buf, l_buf, acc, a_sem, l_sem, weight)
+    own.wait()
+    sofar.wait()
+    factor = pattern[2 * (l * NY + y) + j, z * NH + h].astype(jnp.float32)
+    half = dot3(halves(l_buf[9] * factor), halves(acc[...] + sums[...]))
     acc[...] = half
     for n, (i, k) in enumerate(UPPER):
         rows_of, cols_of = slice(i * q, (i + 1) * q), slice(k * q, (k + 1) * q)
         out[pl.ds((n // 2) * q, q), pl.ds((n % 2) * q, q)] = acc[rows_of, cols_of] + acc[cols_of, rows_of].T
 
 
-def couple(pattern, a_list, l_list):
+def buffers(p, l_count):
+    return [
+        pltpu.VMEM((9, p + 8, p), jnp.float32),
+        pltpu.VMEM((l_count, p, p), jnp.float32),
+    ]
+
+
+def copies():
+    return [pltpu.SemaphoreType.DMA((8,)), pltpu.SemaphoreType.DMA((9,))]
+
+
+def couple_early(pattern, a_list, l_list):
     p = l_list[0].shape[0]
     anywhere = pl.BlockSpec(memory_space=pl.ANY)
     return pl.pallas_call(
-        couple_kernel,
+        early_kernel,
+        out_shape=jax.ShapeDtypeStruct((p, p), jnp.float32),
+        in_specs=[pl.BlockSpec(memory_space=pltpu.SMEM)] + [anywhere] * (len(EARLY_A) + len(EARLY_L)),
+        out_specs=pl.BlockSpec(memory_space=pltpu.VMEM),
+        scratch_shapes=buffers(p, 9) + copies() + [pltpu.SMEM((16,), jnp.int32)],
+        compiler_params=pltpu.CompilerParams(vmem_limit_bytes=40 << 20),
+        cost_estimate=pl.CostEstimate(flops=30 * p**3, bytes_accessed=11 * p * p * 4, transcendentals=0),
+        name="couple_early",
+    )(pattern, *[a_list[k] for k in EARLY_A], *[l_list[k] for k in EARLY_L])
+
+
+def couple_late(pattern, before, a_list, l_list):
+    p = l_list[0].shape[0]
+    anywhere = pl.BlockSpec(memory_space=pl.ANY)
+    return pl.pallas_call(
+        late_kernel,
         out_shape=jax.ShapeDtypeStruct((5 * (p // 4), p // 2), jnp.float32),
-        in_specs=[pl.BlockSpec(memory_space=pltpu.SMEM)] + [anywhere] * (len(a_list) + len(l_list)),
+        in_specs=[pl.BlockSpec(memory_space=pltpu.SMEM)] + [anywhere] * (1 + len(a_list) + len(l_list)),
         out_specs=pl.BlockSpec(memory_space=pltpu.VMEM),
-        scratch_shapes=[
-            pltpu.VMEM((9, p + 8, p), jnp.float32),
-            pltpu.VMEM((10, p, p), jnp.float32),
-            pltpu.VMEM((p, p), jnp.float32),
-            pltpu.SemaphoreType.DMA((8,)),
-            pltpu.SemaphoreType.DMA((10,)),
-            pltpu.SMEM((10,), jnp.int32),
-        ],
+        scratch_shapes=buffers(p, 10)
+        + [pltpu.VMEM((p, p), jnp.float32)] * 2
+        + copies()
+        + [pltpu.SemaphoreType.DMA((2,)), pltpu.SMEM((16,), jnp.int32)],
         compiler_params=pltpu.CompilerParams(vmem_limit_bytes=40 << 20),
-        cost_estimate=pl.CostEstimate(flops=60 * p**3, bytes_accessed=19 * p * p * 4, transcendentals=0),
-        name="couple",
-    )(pattern, *a_list, *l_list)
+        cost_estimate=pl.CostEstimate(flops=40 * p**3, bytes_accessed=13 * p * p * 4, transcendentals=0),
+        name="couple_late",
+    )(pattern, before, *a_list, *l_list)
 
 
 def thirds(x):
@@ -209,11 +268,13 @@
     return jnp.dot(x, y, preferred_element_type=jnp.float32)
 
 
-def slot_kernel(panels, values, slotted, places):
+def slot_kernel(panels, values, *outs):
+    slotted, places = outs[0:8], outs[8]
     items = panels.shape[1]
-    slots = slotted.shape[0]
     n_panels = 8
-    capacity = slots // n_panels
+    capacity = slotted[0].shape[0]
+    slots = n_panels * capacity
+    z, h = coordinates()[0:2]
     before = indicator(
         lax.broadcasted_iota(jnp.int32, (items, items), 0) < lax.broadcasted_iota(jnp.int32, (items, items), 1)
     ).astype(jnp.bfloat16)
@@ -228,33 +289,34 @@
         base = base + jnp.sum(member, axis=1, keepdims=True)
         place = jnp.sum(member * rank, axis=0, keepdims=True).astype(jnp.int32)
         places[k : k + 1, :] = place
-        chosen = indicator(slot_of == panel * capacity + place).astype(jnp.bfloat16)
+        away = jnp.bitwise_and(panel // NH - z + NZ, NZ - 1) * NH + jnp.bitwise_xor(jnp.bitwise_and(panel, NH - 1), h)
+        chosen = indicator(slot_of == away * capacity + place).astype(jnp.bfloat16)
         for piece in thirds(values[:, k, :]):
             part = nn(chosen, piece)
             total = part if total is None else total + part
-    slotted[...] = total
+    for k in range(n_panels):
+        slotted[k][...] = total[k * capacity : (k + 1) * capacity]
 
 
 def slot_entries(panels, values, capacity):
     items, _, p = values.shape
     return pl.pallas_call(
         slot_kernel,
-        out_shape=(
-            jax.ShapeDtypeStruct((8 * capacity, p), jnp.float32),
-            jax.ShapeDtypeStruct((2, items), jnp.int32),
-        ),
+        out_shape=(jax.ShapeDtypeStruct((capacity, p), jnp.float32),) * 8
+        + (jax.ShapeDtypeStruct((2, items), jnp.int32),),
         in_specs=[pl.BlockSpec(memory_space=pltpu.VMEM)] * 2,
-        out_specs=(pl.BlockSpec(memory_space=pltpu.VMEM),) * 2,
+        out_specs=(pl.BlockSpec(memory_space=pltpu.VMEM),) * 9,
         cost_estimate=pl.CostEstimate(flops=12 * capacity * 8 * items * p, bytes_accessed=12 * items * p * 4, transcendentals=0),
         name="slot_entries",
     )(panels, values)
 
 
-def forms_kernel(packed, d, x, out, forms):
+def forms_kernel(packed, d, *refs):
+    xs, (out, forms) = refs[0:8], refs[8:10]
     p = d.shape[0]
     q = p // 4
     capacity = forms.shape[1]
-    step = 4 * capacity
+    z, h = coordinates()[0:2]
     for n, (i, j) in enumerate(UPPER):
         rows, cols = slice(i * q, (i + 1) * q), slice(j * q, (j + 1) * q)
         block = packed[pl.ds((n // 2) * q, q), pl.ds((n % 2) * q, q)]
@@ -263,16 +325,18 @@
             out[cols, rows] = d[cols, rows] + block.T
     high, low = halves(out[...])
     for first in range(2):
-        here = x[first * step : (first + 1) * step, :]
+        here = jnp.concatenate([x[...] for x in xs[4 * first : 4 * first + 4]], axis=0)
         x_high, x_low = halves(here)
         terms = (nn(x_high, high) + (nn(x_high, low) + nn(x_low, high))) * here
         lanes = terms[:, 0:q] + terms[:, q : 2 * q] + (terms[:, 2 * q : 3 * q] + terms[:, 3 * q :])
-        for panel in range(4):
-            mine = lanes[panel * capacity : (panel + 1) * capacity, :]
-            forms[pl.ds(first * 4 + panel, 1), :] = jnp.sum(mine.T, axis=0, keepdims=True)
-
-
-def forms_of(packed, d, x, capacity):
+        for n in range(4):
+            k = 4 * first + n
+            mine = lanes[n * capacity : (n + 1) * capacity, :]
+            source = lax.rem(z - k // NH + NZ, NZ) * NH + (h ^ (k % NH))
+            forms[pl.ds(source, 1), :] = jnp.sum(mine.T, axis=0, keepdims=True)
+
+
+def forms_of(packed, d, xs, capacity):
     p = d.shape[0]
     return pl.pallas_call(
         forms_kernel,
@@ -280,11 +344,11 @@
             jax.ShapeDtypeStruct(d.shape, jnp.float32),
             jax.ShapeDtypeStruct((8, capacity), jnp.float32),
         ),
-        in_specs=[pl.BlockSpec(memory_space=pltpu.VMEM)] * 3,
+        in_specs=[pl.BlockSpec(memory_space=pltpu.VMEM)] * 10,
         out_specs=(pl.BlockSpec(memory_space=pltpu.VMEM),) * 2,
         cost_estimate=pl.CostEstimate(flops=48 * capacity * p * p, bytes_accessed=20 * p * p, transcendentals=0),
         name="forms",
-    )(packed, d, x)
+    )(packed, d, *xs)
 
 
 def finish_kernel(panels, places, answers, out):
@@ -350,18 +414,20 @@
     a1p = lax.ppermute(a1, "row", z_shift(-1))
     l1f = lax.ppermute(l1p, "col", y_shift(-1, keep))
     a1f = lax.ppermute(a0f, "row", H_SWAP)
-    slotted, places = slot_entries(panels, jac_values, capacity)
-    slots_in = exchange(slotted.reshape(n_row, capacity, p), "row")
-    partial_value = couple(
-        pattern,
-        [a0, a0m, a0p, a0f, a1, a1m, a1p, a1f],
-        [l0, l0m, l0p, l0f, l1, l1m, l1p, l1f, l_core],
-    )
+    a_list = [a0, a0m, a0p, a0f, a1, a1m, a1p, a1f]
+    l_list = [l0, l0m, l0p, l0f, l1, l1m, l1p, l1f, l_core]
+    before = couple_early(pattern, a_list, l_list)
+    partial_value = couple_late(pattern, before, a_list, l_list)
+    *slotted, places = slot_entries(panels, jac_values, capacity)
+    xs = [slotted[0]]
+    for k in range(1, 8):
+        moves = [(row_of(z, h), row_of(z + k // NH, h ^ (k % NH))) for z in range(NZ) for h in range(NH)]
+        xs.append(lax.ppermute(slotted[k], "row", moves))
     pieces = partial_value.reshape(n_col, -1, p // 2)
     pieces = exchange(pieces, "col")
     own = jnp.sum(pieces, axis=0)
     whole = exchange(jnp.broadcast_to(own[None], pieces.shape), "col")
-    diag_block, forms = forms_of(whole.reshape(partial_value.shape), d_inverse, slots_in.reshape(-1, p), capacity)
+    diag_block, forms = forms_of(whole.reshape(partial_value.shape), d_inverse, xs, capacity)
     answers = exchange(forms, "row")
     variance = finish(panels, places, answers).reshape(-1)
     return (diag_block, variance)

time: 196 us -> 187 us (0.954)
  waiting for transfers between devices: 92.8 us -> 61.4 us
  starting transfers between devices: 31.9 us -> 49 us
  blocking collectives: 26.2 us -> 29.9 us
    all_to_all x2 -> x1, waiting for transfers between devices: 29.7 us -> 0.01 us  [exchange(): return lax.all_to_all(x, axis, split_axis=0, concat_axis=0, tiled=True)]
    ppermute x0 -> x7, starting transfers between devices: none -> 21 us  [body(): xs.append(lax.ppermute(slotted[k], 'row', moves))]
    ppermute x0 -> x7, waiting for transfers between devices: none -> 12.1 us  [body(): xs.append(lax.ppermute(slotted[k], 'row', moves))]
    ppermute x1, waiting for transfers between devices: 20.8 us -> 10.2 us  [body(): l0f = lax.ppermute(l0m, 'col', y_shift(1, turn_low))]
    ppermute x1, waiting for transfers between devices: 21.1 us -> 17.1 us  [body(): l1 = lax.ppermute(l0, 'col', L_SWAP)]
    all_to_all x2, blocking collectives: 26.2 us -> 29.9 us  [exchange(): return lax.all_to_all(x, axis, split_axis=0, concat_axis=0, tiled=True)]
    all_to_all x2 -> x1, starting transfers between devices: 9.21 us -> 5.6 us  [exchange(): return lax.all_to_all(x, axis, split_axis=0, concat_axis=0, tiled=True)]
    pallas_call x2 -> x3, Pallas kernels: 22.8 us -> 24.5 us  [the longest x1 9.52 us: couple_late(): pl.pallas_call(late_kernel, out_shape=jax.ShapeDtypeStruct((5 * (p // 4),...]
  transfers between devices with their start and end apart: 17 -> 23, of which waited for: 7 -> 10; matrix products, arithmetic and copies ran while one was open for 0% -> 0% of each run, Pallas kernels for 5% -> 8%
where the time goes in v1:
time: 187 us; the launch traced here: 186 us
  waiting for transfers between devices  61.4 us (33%)
  starting transfers between devices  49 us (26%)
  Pallas kernels  33.3 us (18%)
  blocking collectives  29.9 us (16%)
  local copies, waits for them, and re-layouts  11.9 us (6%)
    all_to_all x2, blocking collectives, exchange(): return lax.all_to_all(x, axis, split_axis=0, concat_axis=0, tiled=True)  29.9 us
    ppermute x7, starting transfers between devices, body(): xs.append(lax.ppermute(slotted[k], 'row', moves))  21 us
    ppermute x1, waiting for transfers between devices, body(): a1 = lax.ppermute(a0, 'row', H_SWAP)  17.6 us
    ppermute x1, waiting for transfers between devices, body(): l1 = lax.ppermute(l0, 'col', L_SWAP)  17.1 us
    ppermute x7, waiting for transfers between devices, body(): xs.append(lax.ppermute(slotted[k], 'row', moves))  12.1 us
    unnamed x49, local copies, waits for them, and re-layouts  11.1 us
    ppermute x1, waiting for transfers between devices, body(): l0f = lax.ppermute(l0m, 'col', y_shift(1, turn_low))  10.2 us
    pallas_call x1, Pallas kernels, couple_late(): pl.pallas_call(late_kernel, out_shape=jax.ShapeDtypeStruct((5 * (p // 4),...  9.52 us
  transfers between devices with their start and end apart: 23, of which 10 were waited for; matrix products, arithmetic and copies ran while one was open for 0% of the time, Pallas kernels for 8%

profile of v1, /device:TPU:24, one launch (start us, length us, event | category | flops | bytes accessed | tf_op | source)
XLA Modules:
  0.0 186.5 jit_solution(586888200679261787)
XLA Ops:
  0.6 2.7 %pick.1.refs_0_ = f32[520,512]{1,0:T(8,128)} custom-call(f32[1024,512]{1,0:T(8,128)} %a.1), custom_call_target="tpu_custom_call" | custom-call | bytes 3145728 | tf_op jit(solution)/shard_map/pick/pallas_call | solution.py:97
  7.4 2.5 %collective-permute-start.4 = (f32[512,512]{1,0:T(8,128)}, f32[512,512]{1,0:T(8,128)}, u32[]{:S(2)}, u32[]{:S(2)}) collective-permute-start(f32[512,512]{1,0:T(8,128)} %refs_8_.1), channel_id=1, source_target_pairs={{0,2},{1,3},{2,4},{3,5},{4,6},{5,7},{6,0},{7,1},{8,10},{9,11},{10,... | collective-permute-start | bytes 3145736 | tf_op jit(solution)/shard_map/ppermute | solution.py:402
  10.8 2.7 %collective-permute-start.3 = (f32[520,512]{1,0:T(8,128)}, f32[520,512]{1,0:T(8,128)S(1)}, u32[]{:S(2)}, u32[]{:S(2)}) collective-permute-start(f32[520,512]{1,0:T(8,128)} %pick.1.refs_0_), channel_id=1, source_target_pairs={{0,16},{16,0},{32,48},{48,32},{64,80},{80,64},{96,112},{112,96},{1... | collective-permute-start | bytes 3194888 | tf_op jit(solution)/shard_map/ppermute | solution.py:408
  13.6 17.1 %collective-permute-done.6.refs_8_.refs_12_ = f32[512,512]{1,0:T(8,128)S(1)} collective-permute-done((f32[512,512]{1,0:T(8,128)}, f32[512,512]{1,0:T(8,128)S(1)}, u32[]{:S(2)}, u32[]{:S(2)}) %collective-permute-start.6) | collective-permute-done | bytes 1048608 | tf_op jit(solution)/shard_map/ppermute | solution.py:401
  30.7 2.3 %collective-permute-start.1 = (f32[520,512]{1,0:T(8,128)}, f32[520,512]{1,0:T(8,128)S(1)}, u32[]{:S(2)}, u32[]{:S(2)}) collective-permute-start(f32[520,512]{1,0:T(8,128)} %pick.1.refs_0_), channel_id=1, source_target_pairs={{0,96},{16,112},{32,0},{48,16},{64,32},{80,48},{96,64},{112,80},{1... | collective-permute-start | bytes 3194888 | tf_op jit(solution)/shard_map/ppermute | solution.py:406
  34.7 2.8 %collective-permute-start.7 = (f32[512,512]{1,0:T(8,128)S(1)}, f32[512,512]{1,0:T(8,128)S(1)}, u32[]{:S(2)}, u32[]{:S(2)}) collective-permute-start(f32[512,512]{1,0:T(8,128)S(1)} %collective-permute-done.6.refs_8_.refs_12_), channel_id=1, source_target_pairs={{0,2},{1,3},{2,4},{3,5},{4,6},{5,7},{6,0},{7,1},{8,10},{9,11},{10,... | collective-permute-start | bytes 3145736 | tf_op jit(solution)/shard_map/ppermute | solution.py:409
  38.5 17.6 %collective-permute-done.3.refs_4_ = f32[520,512]{1,0:T(8,128)S(1)} collective-permute-done((f32[520,512]{1,0:T(8,128)}, f32[520,512]{1,0:T(8,128)S(1)}, u32[]{:S(2)}, u32[]{:S(2)}) %collective-permute-start.3) | collective-permute-done | bytes 1064992 | tf_op jit(solution)/shard_map/ppermute | solution.py:408
  56.1 2.2 %collective-permute-start.11 = (f32[520,512]{1,0:T(8,128)S(1)}, f32[520,512]{1,0:T(8,128)}, u32[]{:S(2)}, u32[]{:S(2)}) collective-permute-start(f32[520,512]{1,0:T(8,128)S(1)} %collective-permute-done.3.refs_4_), channel_id=1, source_target_pairs={{0,96},{16,112},{32,0},{48,16},{64,32},{80,48},{96,64},{112,80},{1... | collective-permute-start | bytes 3194888 | tf_op jit(solution)/shard_map/ppermute | solution.py:414
  60.6 2.7 %collective-permute-start.12 = (f32[520,512]{1,0:T(8,128)}, f32[520,512]{1,0:T(8,128)}, u32[]{:S(2)}, u32[]{:S(2)}) collective-permute-start(f32[520,512]{1,0:T(8,128)} %collective-permute-done.2.refs_3_), channel_id=1, source_target_pairs={{0,16},{16,0},{32,48},{48,32},{64,80},{80,64},{96,112},{112,96},{1... | collective-permute-start | bytes 3194888 | tf_op jit(solution)/shard_map/ppermute | solution.py:416
  64.3 2.0 %collective-permute-start.14 = (f32[512,512]{1,0:T(8,128)}, f32[512,512]{1,0:T(8,128)}, u32[]{:S(2)}, u32[]{:S(2)}) collective-permute-start(f32[512,512]{1,0:T(8,128)} %collective-permute-done.8.refs_10_.refs_14_), channel_id=1, source_target_pairs={{0,6},{1,7},{2,0},{3,1},{4,2},{5,3},{6,4},{7,5},{8,14},{9,15},{10,... | collective-permute-start | bytes 3145736 | tf_op jit(solution)/shard_map/ppermute | solution.py:415
  72.5 5.9 %couple_early.1.before = f32[512,512]{1,0:T(8,128)S(1)} custom-call(s32[16,8]{1,0:T(8,128)S(1)} %copy.11.pattern, f32[520,512]{1,0:T(8,128)S(1)} %copy-done, f32[520,512]{1,0:T(8,128)S(1)} %collective-permute-done.refs_1_, f32[520,512]{1,0:T(8,128)S(1)} %collective-permute-done.1.refs_2_, f32[520,512]{1,0:T(8,128)} %collective-permute-done.2.refs_3_, ...), custom_call_target="tpu_custom_call" | custom-call | flops 4026531840 | bytes 11534336 | tf_op jit(solution)/shard_map/couple_early/pallas_call | solution.py:226
  78.4 10.2 %collective-permute-done.13.refs_11_ = f32[512,512]{1,0:T(8,128)} collective-permute-done((f32[512,512]{1,0:T(8,128)}, f32[512,512]{1,0:T(8,128)}, u32[]{:S(2)}, u32[]{:S(2)}) %collective-permute-start.13) | collective-permute-done | bytes 1048608 | tf_op jit(solution)/shard_map/ppermute | solution.py:412
  88.7 2.5 %collective-permute-done.14.refs_15_ = f32[512,512]{1,0:T(8,128)} collective-permute-done((f32[512,512]{1,0:T(8,128)}, f32[512,512]{1,0:T(8,128)}, u32[]{:S(2)}, u32[]{:S(2)}) %collective-permute-start.14) | collective-permute-done | bytes 1048608 | tf_op jit(solution)/shard_map/ppermute | solution.py:415
  91.2 9.5 %couple_late.1 = f32[640,256]{1,0:T(8,128)S(1)} custom-call(s32[16,8]{1,0:T(8,128)S(1)} %copy.11.pattern, f32[512,512]{1,0:T(8,128)S(1)} %couple_early.1.before, f32[520,512]{1,0:T(8,128)S(1)} %copy-done.1, f32[520,512]{1,0:T(8,128)S(1)} %collective-permute-done.refs_1_, f32[520,512]{1,0:T(8,128)S(1)} %collective-permute-done.1.refs_2_, ...), custom_call_target="tpu_custom_call" | custom-call | flops 5368709120 | bytes 13631488 | tf_op jit(solution)/shard_map/couple_late/pallas_call | solution.py:241
  100.7 14.5 %all_to_all.21 = f32[16,40,256]{2,1,0:T(8,128)S(1)} all-to-all(f32[16,40,256]{2,1,0:T(8,128)S(1)} %bitcast.8), channel_id=1, replica_groups=mesh['row'=8,'col'=16] {'col'}, dimensions={0} | all-to-all | bytes 1310720 | tf_op jit(solution)/shard_map/all_to_all | solution.py:380
  116.1 5.6 %all-to-all-start.1 = ((f32[16,40,256]{2,1,0:T(8,128)}), f32[16,40,256]{2,1,0:T(8,128)S(1)}, u32[]{:S(2)}, u32[]{:S(2)}) async-start(f32[16,40,256]{2,1,0:T(8,128)} %broadcast_in_dim.2), calls=%async_computation.1 | async-start | bytes 1310720 | tf_op jit(solution)/shard_map/all_to_all | solution.py:380
  121.7 9.0 %slot_entries.1 = (f32[128,512]{1,0:T(8,128)}, f32[128,512]{1,0:T(8,128)}, f32[128,512]{1,0:T(8,128)}, f32[128,512]{1,0:T(8,128)}, f32[128,512]{1,0:T(8,128)}, /...) custom-call(s32[2,256]{1,0:T(2,128)} %bitcast.12, f32[256,2,512]{2,1,0:T(2,128)} %values.1), custom_call_target="tpu_custom_call" | custom-call | flops 1610612736 | bytes 6291456 | tf_op jit(solution)/shard_map/slot_entries/pallas_call | solution.py:303
  132.4 2.9 %collective-permute-start.17 = (f32[128,512]{1,0:T(8,128)}, f32[128,512]{1,0:T(8,128)S(1)}, u32[]{:S(2)}, u32[]{:S(2)}) collective-permute-start(f32[128,512]{1,0:T(8,128)} %get-tuple-element.16), channel_id=1, source_target_pairs={{0,48},{16,32},{32,80},{48,64},{64,112},{80,96},{96,16},{112,0},{1... | collective-permute-start | bytes 786440 | tf_op jit(solution)/shard_map/ppermute | solution.py:425
  135.3 3.1 %collective-permute-start.18 = (f32[128,512]{1,0:T(8,128)}, f32[128,512]{1,0:T(8,128)S(1)}, u32[]{:S(2)}, u32[]{:S(2)}) collective-permute-start(f32[128,512]{1,0:T(8,128)} %get-tuple-element.17), channel_id=1, source_target_pairs={{0,64},{16,80},{32,96},{48,112},{64,0},{80,16},{96,32},{112,48},{1... | collective-permute-start | bytes 786440 | tf_op jit(solution)/shard_map/ppermute | solution.py:425
  141.7 6.2 %collective-permute-done.16.refs_2_ = f32[128,512]{1,0:T(8,128)S(1)} collective-permute-done((f32[128,512]{1,0:T(8,128)}, f32[128,512]{1,0:T(8,128)S(1)}, u32[]{:S(2)}, u32[]{:S(2)}) %collective-permute-start.16) | collective-permute-done | bytes 262176 | tf_op jit(solution)/shard_map/ppermute | solution.py:425
  147.9 11.8 %collective-permute-start.21 = (f32[128,512]{1,0:T(8,128)}, f32[128,512]{1,0:T(8,128)S(1)}, u32[]{:S(2)}, u32[]{:S(2)}) collective-permute-start(f32[128,512]{1,0:T(8,128)} %get-tuple-element.20), channel_id=1, source_target_pairs={{0,112},{16,96},{32,16},{48,0},{64,48},{80,32},{96,80},{112,64},{1... | collective-permute-start | bytes 786440 | tf_op jit(solution)/shard_map/ppermute | solution.py:425
  160.7 3.3 %collective-permute-done.21.refs_7_ = f32[128,512]{1,0:T(8,128)S(1)} collective-permute-done((f32[128,512]{1,0:T(8,128)}, f32[128,512]{1,0:T(8,128)S(1)}, u32[]{:S(2)}, u32[]{:S(2)}) %collective-permute-start.21) | collective-permute-done | bytes 262176 | tf_op jit(solution)/shard_map/ppermute | solution.py:425
  164.9 4.7 %forms.1 = (f32[512,512]{1,0:T(8,128)}, f32[8,128]{1,0:T(8,128)}) custom-call(f32[640,256]{1,0:T(8,128)} %bitcast.9, f32[512,512]{1,0:T(8,128)} %d.1, f32[128,512]{1,0:T(8,128)} %get-tuple-element.13.refs_0_, f32[128,512]{1,0:T(8,128)} %copy-done.17, f32[128,512]{1,0:T(8,128)} %copy-done.18, f32[128,512]{1,0:T(8,128)} %copy-done.19, f32[128,512]{1,0:T(8,128)} %copy-done.20, ...), custom_call_target="tpu_custom_call" | custom-call | flops 1610612736 | bytes 5242880 | tf_op jit(solution)/shard_map/forms/pallas_call | solution.py:341
  169.6 15.4 %all_to_all.22 = f32[8,1,128]{2,1,0:T(1,128)} all-to-all(f32[8,1,128]{2,1,0:T(1,128)} %bitcast.11), channel_id=1, replica_groups=mesh['row'=8,'col'=16] {'row'}, dimensions={0} | all-to-all | bytes 8192 | tf_op jit(solution)/shard_map/all_to_all | solution.py:380
  (81 shorter events, 26.2 us)
Async XLA Ops:
  0.6 65.7 %copy-start.16 = (s32[16,8]{0,1:T(8,128)S(1)}, s32[16,8]{0,1:T(8,128)}, u32[]{:S(2)}) copy-start(s32[16,8]{0,1:T(8,128)} %param.8) | copy-start | bytes 1540
  3.3 29.6 %collective-permute-start = (f32[520,512]{1,0:T(8,128)}, f32[520,512]{1,0:T(8,128)S(1)}, u32[]{:S(2)}, u32[]{:S(2)}) collective-permute-start(f32[520,512]{1,0:T(8,128)} %pick.1.refs_0_), channel_id=1, source_target_pairs={{0,32},{16,48},{32,64},{48,80},{64,96},{80,112},{96,0},{112,16},{1... | collective-permute-start | bytes 3194888 | tf_op jit(solution)/shard_map/ppermute | solution.py:405
  5.3 4.6 %collective-permute-start.9 = (f32[512,512]{1,0:T(8,128)}, f32[512,512]{1,0:T(8,128)S(1)}, u32[]{:S(2)}, u32[]{:S(2)}) collective-permute-start(f32[512,512]{1,0:T(8,128)} %refs_8_.1), channel_id=1, source_target_pairs={{0,1},{1,0},{2,3},{3,2},{4,5},{5,4},{6,7},{7,6},{8,9},{9,8},{10,11... | collective-permute-start | bytes 3145736 | tf_op jit(solution)/shard_map/ppermute | solution.py:407
  5.3 25.4 %collective-permute-start.6 = (f32[512,512]{1,0:T(8,128)}, f32[512,512]{1,0:T(8,128)S(1)}, u32[]{:S(2)}, u32[]{:S(2)}) collective-permute-start(f32[512,512]{1,0:T(8,128)} %refs_8_.1), channel_id=1, source_target_pairs={{0,8},{1,9},{2,10},{3,11},{4,12},{5,13},{6,14},{7,15},{8,1},{9,0},... | collective-permute-start | bytes 3145736 | tf_op jit(solution)/shard_map/ppermute | solution.py:401
  6.8 26.5 %collective-permute-start.5 = (f32[512,512]{1,0:T(8,128)}, f32[512,512]{1,0:T(8,128)S(1)}, u32[]{:S(2)}, u32[]{:S(2)}) collective-permute-start(f32[512,512]{1,0:T(8,128)} %refs_8_.1), channel_id=1, source_target_pairs={{0,7},{1,6},{2,1},{3,0},{4,3},{5,2},{6,5},{7,4},{8,15},{9,14},{10,... | collective-permute-start | bytes 3145736 | tf_op jit(solution)/shard_map/ppermute | solution.py:403
  7.4 27.3 %collective-permute-start.4 = (f32[512,512]{1,0:T(8,128)}, f32[512,512]{1,0:T(8,128)}, u32[]{:S(2)}, u32[]{:S(2)}) collective-permute-start(f32[512,512]{1,0:T(8,128)} %refs_8_.1), channel_id=1, source_target_pairs={{0,2},{1,3},{2,4},{3,5},{4,6},{5,7},{6,0},{7,1},{8,10},{9,11},{10,... | collective-permute-start | bytes 3145736 | tf_op jit(solution)/shard_map/ppermute | solution.py:402
  10.8 45.3 %collective-permute-start.3 = (f32[520,512]{1,0:T(8,128)}, f32[520,512]{1,0:T(8,128)S(1)}, u32[]{:S(2)}, u32[]{:S(2)}) collective-permute-start(f32[520,512]{1,0:T(8,128)} %pick.1.refs_0_), channel_id=1, source_target_pairs={{0,16},{16,0},{32,48},{48,32},{64,80},{80,64},{96,112},{112,96},{1... | collective-permute-start | bytes 3194888 | tf_op jit(solution)/shard_map/ppermute | solution.py:408
  30.7 27.7 %collective-permute-start.1 = (f32[520,512]{1,0:T(8,128)}, f32[520,512]{1,0:T(8,128)S(1)}, u32[]{:S(2)}, u32[]{:S(2)}) collective-permute-start(f32[520,512]{1,0:T(8,128)} %pick.1.refs_0_), channel_id=1, source_target_pairs={{0,96},{16,112},{32,0},{48,16},{64,32},{80,48},{96,64},{112,80},{1... | collective-permute-start | bytes 3194888 | tf_op jit(solution)/shard_map/ppermute | solution.py:406
  33.0 27.6 %collective-permute-start.2 = (f32[520,512]{1,0:T(8,128)S(1)}, f32[520,512]{1,0:T(8,128)}, u32[]{:S(2)}, u32[]{:S(2)}) collective-permute-start(f32[520,512]{1,0:T(8,128)S(1)} %collective-permute-done.refs_1_), channel_id=1, source_target_pairs={{0,32},{16,48},{32,64},{48,80},{64,96},{80,112},{96,0},{112,16},{1... | collective-permute-start | bytes 3194888 | tf_op jit(solution)/shard_map/ppermute | solution.py:411
  34.2 29.0 %collective-permute-start.8 = (f32[512,512]{1,0:T(8,128)S(1)}, f32[512,512]{1,0:T(8,128)}, u32[]{:S(2)}, u32[]{:S(2)}) collective-permute-start(f32[512,512]{1,0:T(8,128)S(1)} %collective-permute-done.6.refs_8_.refs_12_), channel_id=1, source_target_pairs={{0,6},{1,7},{2,0},{3,1},{4,2},{5,3},{6,4},{7,5},{8,14},{9,15},{10,... | collective-permute-start | bytes 3145736 | tf_op jit(solution)/shard_map/ppermute | solution.py:410
  34.7 28.6 %collective-permute-start.7 = (f32[512,512]{1,0:T(8,128)S(1)}, f32[512,512]{1,0:T(8,128)S(1)}, u32[]{:S(2)}, u32[]{:S(2)}) collective-permute-start(f32[512,512]{1,0:T(8,128)S(1)} %collective-permute-done.6.refs_8_.refs_12_), channel_id=1, source_target_pairs={{0,2},{1,3},{2,4},{3,5},{4,6},{5,7},{6,0},{7,1},{8,10},{9,11},{10,... | collective-permute-start | bytes 3145736 | tf_op jit(solution)/shard_map/ppermute | solution.py:409
  56.1 32.5 %collective-permute-start.11 = (f32[520,512]{1,0:T(8,128)S(1)}, f32[520,512]{1,0:T(8,128)}, u32[]{:S(2)}, u32[]{:S(2)}) collective-permute-start(f32[520,512]{1,0:T(8,128)S(1)} %collective-permute-done.3.refs_4_), channel_id=1, source_target_pairs={{0,96},{16,112},{32,0},{48,16},{64,32},{80,48},{96,64},{112,80},{1... | collective-permute-start | bytes 3194888 | tf_op jit(solution)/shard_map/ppermute | solution.py:414
  58.4 30.3 %collective-permute-start.10 = (f32[520,512]{1,0:T(8,128)S(1)}, f32[520,512]{1,0:T(8,128)}, u32[]{:S(2)}, u32[]{:S(2)}) collective-permute-start(f32[520,512]{1,0:T(8,128)S(1)} %collective-permute-done.3.refs_4_), channel_id=1, source_target_pairs={{0,32},{16,48},{32,64},{48,80},{64,96},{80,112},{96,0},{112,16},{1... | collective-permute-start | bytes 3194888 | tf_op jit(solution)/shard_map/ppermute | solution.py:413
  60.6 30.6 %collective-permute-start.12 = (f32[520,512]{1,0:T(8,128)}, f32[520,512]{1,0:T(8,128)}, u32[]{:S(2)}, u32[]{:S(2)}) collective-permute-start(f32[520,512]{1,0:T(8,128)} %collective-permute-done.2.refs_3_), channel_id=1, source_target_pairs={{0,16},{16,0},{32,48},{48,32},{64,80},{80,64},{96,112},{112,96},{1... | collective-permute-start | bytes 3194888 | tf_op jit(solution)/shard_map/ppermute | solution.py:416
  63.3 25.4 %collective-permute-start.13 = (f32[512,512]{1,0:T(8,128)}, f32[512,512]{1,0:T(8,128)}, u32[]{:S(2)}, u32[]{:S(2)}) collective-permute-start(f32[512,512]{1,0:T(8,128)} %collective-permute-done.4.refs_6_.refs_9_), channel_id=1, source_target_pairs={{0,3},{1,2},{2,4},{3,5},{4,6},{5,7},{6,1},{7,0},{8,11},{9,10},{10,... | collective-permute-start | bytes 3145736 | tf_op jit(solution)/shard_map/ppermute | solution.py:412
  64.3 26.9 %collective-permute-start.14 = (f32[512,512]{1,0:T(8,128)}, f32[512,512]{1,0:T(8,128)}, u32[]{:S(2)}, u32[]{:S(2)}) collective-permute-start(f32[512,512]{1,0:T(8,128)} %collective-permute-done.8.refs_10_.refs_14_), channel_id=1, source_target_pairs={{0,6},{1,7},{2,0},{3,1},{4,2},{5,3},{6,4},{7,5},{8,14},{9,15},{10,... | collective-permute-start | bytes 3145736 | tf_op jit(solution)/shard_map/ppermute | solution.py:415
  116.1 47.8 %all-to-all-start.1 = ((f32[16,40,256]{2,1,0:T(8,128)}), f32[16,40,256]{2,1,0:T(8,128)S(1)}, u32[]{:S(2)}, u32[]{:S(2)}) async-start(f32[16,40,256]{2,1,0:T(8,128)} %broadcast_in_dim.2), calls=%async_computation.1 | async-start | bytes 1310720 | tf_op jit(solution)/shard_map/all_to_all | solution.py:380
  130.8 10.9 %collective-permute-start.15 = (f32[128,512]{1,0:T(8,128)}, f32[128,512]{1,0:T(8,128)S(1)}, u32[]{:S(2)}, u32[]{:S(2)}) collective-permute-start(f32[128,512]{1,0:T(8,128)} %get-tuple-element.14), channel_id=1, source_target_pairs={{0,16},{16,0},{32,48},{48,32},{64,80},{80,64},{96,112},{112,96},{1... | collective-permute-start | bytes 786440 | tf_op jit(solution)/shard_map/ppermute | solution.py:425
  131.5 16.3 %collective-permute-start.16 = (f32[128,512]{1,0:T(8,128)}, f32[128,512]{1,0:T(8,128)S(1)}, u32[]{:S(2)}, u32[]{:S(2)}) collective-permute-start(f32[128,512]{1,0:T(8,128)} %get-tuple-element.15), channel_id=1, source_target_pairs={{0,32},{16,48},{32,64},{48,80},{64,96},{80,112},{96,0},{112,16},{1... | collective-permute-start | bytes 786440 | tf_op jit(solution)/shard_map/ppermute | solution.py:425
  132.4 27.3 %collective-permute-start.17 = (f32[128,512]{1,0:T(8,128)}, f32[128,512]{1,0:T(8,128)S(1)}, u32[]{:S(2)}, u32[]{:S(2)}) collective-permute-start(f32[128,512]{1,0:T(8,128)} %get-tuple-element.16), channel_id=1, source_target_pairs={{0,48},{16,32},{32,80},{48,64},{64,112},{80,96},{96,16},{112,0},{1... | collective-permute-start | bytes 786440 | tf_op jit(solution)/shard_map/ppermute | solution.py:425
  135.3 24.4 %collective-permute-start.18 = (f32[128,512]{1,0:T(8,128)}, f32[128,512]{1,0:T(8,128)S(1)}, u32[]{:S(2)}, u32[]{:S(2)}) collective-permute-start(f32[128,512]{1,0:T(8,128)} %get-tuple-element.17), channel_id=1, source_target_pairs={{0,64},{16,80},{32,96},{48,112},{64,0},{80,16},{96,32},{112,48},{1... | collective-permute-start | bytes 786440 | tf_op jit(solution)/shard_map/ppermute | solution.py:425
  138.4 21.3 %collective-permute-start.19 = (f32[128,512]{1,0:T(8,128)}, f32[128,512]{1,0:T(8,128)S(1)}, u32[]{:S(2)}, u32[]{:S(2)}) collective-permute-start(f32[128,512]{1,0:T(8,128)} %get-tuple-element.18), channel_id=1, source_target_pairs={{0,80},{16,64},{32,112},{48,96},{64,16},{80,0},{96,48},{112,32},{1... | collective-permute-start | bytes 786440 | tf_op jit(solution)/shard_map/ppermute | solution.py:425
  141.7 19.0 %collective-permute-start.20 = (f32[128,512]{1,0:T(8,128)}, f32[128,512]{1,0:T(8,128)S(1)}, u32[]{:S(2)}, u32[]{:S(2)}) collective-permute-start(f32[128,512]{1,0:T(8,128)} %get-tuple-element.19), channel_id=1, source_target_pairs={{0,96},{16,112},{32,0},{48,16},{64,32},{80,48},{96,64},{112,80},{1... | collective-permute-start | bytes 786440 | tf_op jit(solution)/shard_map/ppermute | solution.py:425
  147.9 16.1 %collective-permute-start.21 = (f32[128,512]{1,0:T(8,128)}, f32[128,512]{1,0:T(8,128)S(1)}, u32[]{:S(2)}, u32[]{:S(2)}) collective-permute-start(f32[128,512]{1,0:T(8,128)} %get-tuple-element.20), channel_id=1, source_target_pairs={{0,112},{16,96},{32,16},{48,0},{64,48},{80,32},{96,80},{112,64},{1... | collective-permute-start | bytes 786440 | tf_op jit(solution)/shard_map/ppermute | solution.py:425
  (23 other events, 181.6 us)

commit v2 on v1

--- a/solution.py
+++ b/solution.py
@@ -131,7 +131,11 @@
 
             @pl.when(active)
             def _():
-                pltpu.make_async_copy(a_in[k], a_buf.at[k], a_sem.at[k]).start()
+                start = 0
+                for part in a_in[k]:
+                    stop = start + part.shape[0]
+                    pltpu.make_async_copy(part, a_buf.at[k, start:stop], a_sem.at[k]).start()
+                    start = stop
 
             for s in range(8):
                 if s in l_in:
@@ -163,7 +167,7 @@
         def _():
             @pl.when(k < 8)
             def _():
-                pltpu.make_async_copy(a_in[0], a_buf.at[usual], a_sem.at[usual]).wait()
+                pltpu.make_async_copy(a_in[0][0], a_buf.at[usual], a_sem.at[usual]).wait()
 
             pltpu.make_async_copy(l_in[0], l_buf.at[k], l_sem.at[k]).wait()
 
@@ -179,18 +183,30 @@
             acc[...] += dot3(halves(a), halves(l_buf[k]))
 
 
+def grouped(slots, refs):
+    groups = {}
+    for k in slots:
+        count = 2 if k in (3, 7) else 1
+        groups[k], refs = refs[:count], refs[count:]
+    return groups, refs
+
+
+def flat(a_list, slots):
+    return [part for k in slots for part in a_list[k]]
+
+
 def early_kernel(pattern, *refs):
-    count = len(EARLY_A) + len(EARLY_L)
-    a_in = dict(zip(EARLY_A, refs[: len(EARLY_A)]))
-    l_in = dict(zip(EARLY_L, refs[len(EARLY_A) : count]))
+    a_in, refs = grouped(EARLY_A, refs)
+    l_in = dict(zip(EARLY_L, refs))
+    count = len(EARLY_L)
     acc, a_buf, l_buf, a_sem, l_sem, weight = refs[count:]
     add_products(True, pattern, a_in, l_in, a_buf, l_buf, acc, a_sem, l_sem, weight)
 
 
 def late_kernel(pattern, before, *refs):
-    a_in = dict(enumerate(refs[0:8]))
-    l_in = dict(enumerate(refs[8:17]))
-    out, a_buf, l_buf, acc, sums, a_sem, l_sem, more_sem, weight = refs[17:]
+    a_in, refs = grouped(range(8), refs)
+    l_in = dict(enumerate(refs[0:9]))
+    out, a_buf, l_buf, acc, sums, a_sem, l_sem, more_sem, weight = refs[9:]
     p = acc.shape[0]
     q = p // 4
     z, h, l, y, j = coordinates()
@@ -226,13 +242,13 @@
     return pl.pallas_call(
         early_kernel,
         out_shape=jax.ShapeDtypeStruct((p, p), jnp.float32),
-        in_specs=[pl.BlockSpec(memory_space=pltpu.SMEM)] + [anywhere] * (len(EARLY_A) + len(EARLY_L)),
+        in_specs=[pl.BlockSpec(memory_space=pltpu.SMEM)] + [anywhere] * (len(flat(a_list, EARLY_A)) + len(EARLY_L)),
         out_specs=pl.BlockSpec(memory_space=pltpu.VMEM),
         scratch_shapes=buffers(p, 9) + copies() + [pltpu.SMEM((16,), jnp.int32)],
         compiler_params=pltpu.CompilerParams(vmem_limit_bytes=40 << 20),
         cost_estimate=pl.CostEstimate(flops=30 * p**3, bytes_accessed=11 * p * p * 4, transcendentals=0),
         name="couple_early",
-    )(pattern, *[a_list[k] for k in EARLY_A], *[l_list[k] for k in EARLY_L])
+    )(pattern, *flat(a_list, EARLY_A), *[l_list[k] for k in EARLY_L])
 
 
 def couple_late(pattern, before, a_list, l_list):
@@ -241,7 +257,7 @@
     return pl.pallas_call(
         late_kernel,
         out_shape=jax.ShapeDtypeStruct((5 * (p // 4), p // 2), jnp.float32),
-        in_specs=[pl.BlockSpec(memory_space=pltpu.SMEM)] + [anywhere] * (1 + len(a_list) + len(l_list)),
+        in_specs=[pl.BlockSpec(memory_space=pltpu.SMEM)] + [anywhere] * (1 + len(flat(a_list, range(8))) + len(l_list)),
         out_specs=pl.BlockSpec(memory_space=pltpu.VMEM),
         scratch_shapes=buffers(p, 10)
         + [pltpu.VMEM((p, p), jnp.float32)] * 2
@@ -250,7 +266,7 @@
         compiler_params=pltpu.CompilerParams(vmem_limit_bytes=40 << 20),
         cost_estimate=pl.CostEstimate(flops=40 * p**3, bytes_accessed=13 * p * p * 4, transcendentals=0),
         name="couple_late",
-    )(pattern, before, *a_list, *l_list)
+    )(pattern, before, *flat(a_list, range(8)), *l_list)
 
 
 def thirds(x):
@@ -269,7 +285,7 @@
 
 
 def slot_kernel(panels, values, *outs):
-    slotted, places = outs[0:8], outs[8]
+    slotted, across, places = outs[0:4], outs[4], outs[5]
     items = panels.shape[1]
     n_panels = 8
     capacity = slotted[0].shape[0]
@@ -289,23 +305,24 @@
         base = base + jnp.sum(member, axis=1, keepdims=True)
         place = jnp.sum(member * rank, axis=0, keepdims=True).astype(jnp.int32)
         places[k : k + 1, :] = place
-        away = jnp.bitwise_and(panel // NH - z + NZ, NZ - 1) * NH + jnp.bitwise_xor(jnp.bitwise_and(panel, NH - 1), h)
+        away = jnp.bitwise_and(panel // NH - z + NZ, NZ - 1) + NZ * jnp.bitwise_xor(jnp.bitwise_and(panel, NH - 1), h)
         chosen = indicator(slot_of == away * capacity + place).astype(jnp.bfloat16)
         for piece in thirds(values[:, k, :]):
             part = nn(chosen, piece)
             total = part if total is None else total + part
-    for k in range(n_panels):
+    for k in range(NZ):
         slotted[k][...] = total[k * capacity : (k + 1) * capacity]
+    across[...] = total[NZ * capacity :]
 
 
 def slot_entries(panels, values, capacity):
     items, _, p = values.shape
     return pl.pallas_call(
         slot_kernel,
-        out_shape=(jax.ShapeDtypeStruct((capacity, p), jnp.float32),) * 8
-        + (jax.ShapeDtypeStruct((2, items), jnp.int32),),
+        out_shape=(jax.ShapeDtypeStruct((capacity, p), jnp.float32),) * NZ
+        + (jax.ShapeDtypeStruct((NZ * capacity, p), jnp.float32), jax.ShapeDtypeStruct((2, items), jnp.int32)),
         in_specs=[pl.BlockSpec(memory_space=pltpu.VMEM)] * 2,
-        out_specs=(pl.BlockSpec(memory_space=pltpu.VMEM),) * 9,
+        out_specs=(pl.BlockSpec(memory_space=pltpu.VMEM),) * 6,
         cost_estimate=pl.CostEstimate(flops=12 * capacity * 8 * items * p, bytes_accessed=12 * items * p * 4, transcendentals=0),
         name="slot_entries",
     )(panels, values)
@@ -325,14 +342,13 @@
             out[cols, rows] = d[cols, rows] + block.T
     high, low = halves(out[...])
     for first in range(2):
-        here = jnp.concatenate([x[...] for x in xs[4 * first : 4 * first + 4]], axis=0)
+        here = jnp.concatenate([x[0:capacity] for x in xs[4 * first : 4 * first + 4]], axis=0)
         x_high, x_low = halves(here)
         terms = (nn(x_high, high) + (nn(x_high, low) + nn(x_low, high))) * here
         lanes = terms[:, 0:q] + terms[:, q : 2 * q] + (terms[:, 2 * q : 3 * q] + terms[:, 3 * q :])
         for n in range(4):
-            k = 4 * first + n
             mine = lanes[n * capacity : (n + 1) * capacity, :]
-            source = lax.rem(z - k // NH + NZ, NZ) * NH + (h ^ (k % NH))
+            source = lax.rem(z - n + NZ, NZ) * NH + (h ^ first)
             forms[pl.ds(source, 1), :] = jnp.sum(mine.T, axis=0, keepdims=True)
 
 
@@ -408,21 +424,22 @@
     a1 = lax.ppermute(a0, "row", H_SWAP)
     l1m = lax.ppermute(l1, "col", y_shift(1, keep))
     l1p = lax.ppermute(l1, "col", y_shift(-1, keep))
-    a0f = lax.ppermute(a0m, "row", z_shift(1))
+    cut = (p // 16 + 1) * 8
+    a0f = (lax.ppermute(a0m[:cut], "row", z_shift(1)), lax.ppermute(a0p[cut:], "row", z_shift(-1)))
     l0f = lax.ppermute(l0m, "col", y_shift(1, turn_low))
     a1m = lax.ppermute(a1, "row", z_shift(1))
     a1p = lax.ppermute(a1, "row", z_shift(-1))
     l1f = lax.ppermute(l1p, "col", y_shift(-1, keep))
-    a1f = lax.ppermute(a0f, "row", H_SWAP)
-    a_list = [a0, a0m, a0p, a0f, a1, a1m, a1p, a1f]
+    a1f = (lax.ppermute(a0f[0], "row", H_SWAP), lax.ppermute(a0f[1], "row", H_SWAP))
+    a_list = [(a0,), (a0m,), (a0p,), a0f, (a1,), (a1m,), (a1p,), a1f]
     l_list = [l0, l0m, l0p, l0f, l1, l1m, l1p, l1f, l_core]
     before = couple_early(pattern, a_list, l_list)
     partial_value = couple_late(pattern, before, a_list, l_list)
-    *slotted, places = slot_entries(panels, jac_values, capacity)
-    xs = [slotted[0]]
-    for k in range(1, 8):
-        moves = [(row_of(z, h), row_of(z + k // NH, h ^ (k % NH))) for z in range(NZ) for h in range(NH)]
-        xs.append(lax.ppermute(slotted[k], "row", moves))
+    *slotted, across, places = slot_entries(panels, jac_values, capacity)
+    crossed = lax.ppermute(across, "row", H_SWAP)
+    xs = [slotted[0]] + [lax.ppermute(slotted[k], "row", z_shift(k)) for k in range(1, NZ)] + [crossed]
+    for k in range(1, NZ):
+        xs.append(lax.ppermute(crossed[k * capacity : (k + 1) * capacity], "row", z_shift(k)))
     pieces = partial_value.reshape(n_col, -1, p // 2)
     pieces = exchange(pieces, "col")
     own = jnp.sum(pieces, axis=0)

time: 187 us -> 215 us (1.15)
  waiting for transfers between devices: 61.4 us -> 82 us
  blocking collectives: 29.9 us -> 35.3 us
  starting transfers between devices: 49 us -> 51.8 us
    ppermute x1, waiting for transfers between devices: 0.01 us -> 17.8 us  [body(): l1m = lax.ppermute(l1, 'col', y_shift(1, keep))]
    ppermute x1, waiting for transfers between devices: 17.6 us -> 0.01 us  [body(): a1 = lax.ppermute(a0, 'row', H_SWAP)]
    ppermute x1, waiting for transfers between devices: 0.01 us -> 11.1 us  [body(): l0m = lax.ppermute(l0, 'col', y_shift(1, keep))]
    ppermute x1, waiting for transfers between devices: 10.2 us -> 18.1 us  [body(): l0f = lax.ppermute(l0m, 'col', y_shift(1, turn_low))]
    ppermute x9 -> x11, waiting for transfers between devices: 13.7 us -> 6.86 us  [the longest x3 4.91 us: body(): lax.ppermute(crossed[k * capacity:(k + 1) * capacity], 'row', z_shift(k))]
    ppermute x1, waiting for transfers between devices: 0.01 us -> 6.71 us  [body(): a0m = lax.ppermute(a0, 'row', z_shift(1))]
    all_to_all x2, blocking collectives: 29.9 us -> 35.3 us  [exchange(): return lax.all_to_all(x, axis, split_axis=0, concat_axis=0, tiled=True)]
    ppermute x9 -> x11, starting transfers between devices: 23.7 us -> 28 us  [the longest x3 12.4 us: body(): lax.ppermute(crossed[k * capacity:(k + 1) * capacity], 'row', z_shift(k))]
  transfers between devices with their start and end apart: 23 -> 25, of which waited for: 10 -> 10; matrix products, arithmetic and copies ran while one was open for 0% -> 1% of each run, Pallas kernels for 8% -> 13%
where the time goes in v2:
time: 215 us; the launch traced here: 214 us
  waiting for transfers between devices  82 us (38%)
  starting transfers between devices  51.8 us (24%)
  blocking collectives  35.3 us (16%)
  Pallas kernels  33.2 us (15%)
  local copies, waits for them, and re-layouts  11.1 us (5%)
    all_to_all x2, blocking collectives, exchange(): return lax.all_to_all(x, axis, split_axis=0, concat_axis=0, tiled=True)  35.3 us
    ppermute x1, waiting for transfers between devices, body(): l0f = lax.ppermute(l0m, 'col', y_shift(1, turn_low))  18.1 us
    ppermute x1, waiting for transfers between devices, body(): l1m = lax.ppermute(l1, 'col', y_shift(1, keep))  17.8 us
    ppermute x1, waiting for transfers between devices, body(): l1 = lax.ppermute(l0, 'col', L_SWAP)  14.3 us
    ppermute x3, starting transfers between devices, body(): lax.ppermute(crossed[k * capacity:(k + 1) * capacity], 'row', z_shift(k))  12.4 us
    ppermute x1, waiting for transfers between devices, body(): l0m = lax.ppermute(l0, 'col', y_shift(1, keep))  11.1 us
    unnamed x57, local copies, waits for them, and re-layouts  10.1 us
    pallas_call x1, Pallas kernels, couple_late(): pl.pallas_call(late_kernel, out_shape=jax.ShapeDtypeStruct((5 * (p // 4),...  9.22 us
  transfers between devices with their start and end apart: 25, of which 10 were waited for; matrix products, arithmetic and copies ran while one was open for 1% of the time, Pallas kernels for 13%

profile of v2, /device:TPU:24, one launch (start us, length us, event | category | flops | bytes accessed | tf_op | source)
XLA Modules:
  0.0 214.3 jit_solution(14892301197659294097)
XLA Ops:
  2.3 2.6 %pick.1.refs_0_ = f32[520,512]{1,0:T(8,128)} custom-call(f32[1024,512]{1,0:T(8,128)} %a.1), custom_call_target="tpu_custom_call" | custom-call | bytes 3145728 | tf_op jit(solution)/shard_map/pick/pallas_call | solution.py:97
  6.9 2.2 %collective-permute-start.1 = (f32[520,512]{1,0:T(8,128)}, f32[520,512]{1,0:T(8,128)S(1)}, u32[]{:S(2)}, u32[]{:S(2)}) collective-permute-start(f32[520,512]{1,0:T(8,128)} %pick.1.refs_0_), channel_id=1, source_target_pairs={{0,96},{16,112},{32,0},{48,16},{64,32},{80,48},{96,64},{112,80},{1... | collective-permute-start | bytes 3194888 | tf_op jit(solution)/shard_map/ppermute | solution.py:422
  9.1 2.7 %collective-permute-start.4 = (f32[520,512]{1,0:T(8,128)}, f32[520,512]{1,0:T(8,128)}, u32[]{:S(2)}, u32[]{:S(2)}) collective-permute-start(f32[520,512]{1,0:T(8,128)} %pick.1.refs_0_), channel_id=1, source_target_pairs={{0,16},{16,0},{32,48},{48,32},{64,80},{80,64},{96,112},{112,96},{1... | collective-permute-start | bytes 3194888 | tf_op jit(solution)/shard_map/ppermute | solution.py:424
  11.9 14.3 %collective-permute-done.7.refs_9_.refs_14_ = f32[512,512]{1,0:T(8,128)} collective-permute-done((f32[512,512]{1,0:T(8,128)}, f32[512,512]{1,0:T(8,128)}, u32[]{:S(2)}, u32[]{:S(2)}) %collective-permute-start.7) | collective-permute-done | bytes 1048608 | tf_op jit(solution)/shard_map/ppermute | solution.py:417
  26.4 6.7 %collective-permute-done.refs_1_ = f32[520,512]{1,0:T(8,128)S(1)} collective-permute-done((f32[520,512]{1,0:T(8,128)}, f32[520,512]{1,0:T(8,128)S(1)}, u32[]{:S(2)}, u32[]{:S(2)}) %collective-permute-start) | collective-permute-done | bytes 1064992 | tf_op jit(solution)/shard_map/ppermute | solution.py:421
  34.4 4.2 %collective-permute-done.6.refs_8_.refs_12_ = f32[512,512]{1,0:T(8,128)S(1)} collective-permute-done((f32[512,512]{1,0:T(8,128)S(1)}, f32[512,512]{1,0:T(8,128)S(1)}, u32[]{:S(2)}, u32[]{:S(2)}) %collective-permute-start.6) | collective-permute-done | bytes 1048608 | tf_op jit(solution)/shard_map/ppermute | solution.py:419
  41.1 11.1 %collective-permute-done.5.refs_7_.refs_11_ = f32[512,512]{1,0:T(8,128)} collective-permute-done((f32[512,512]{1,0:T(8,128)S(1)}, f32[512,512]{1,0:T(8,128)}, u32[]{:S(2)}, u32[]{:S(2)}) %collective-permute-start.5) | collective-permute-done | bytes 1048608 | tf_op jit(solution)/shard_map/ppermute | solution.py:418
  53.6 4.1 %collective-permute-start.12 = (f32[520,512]{1,0:T(8,128)}, f32[520,512]{1,0:T(8,128)}, u32[]{:S(2)}, u32[]{:S(2)}) collective-permute-start(f32[520,512]{1,0:T(8,128)} %collective-permute-done.4.refs_5_), channel_id=1, source_target_pairs={{0,96},{16,112},{32,0},{48,16},{64,32},{80,48},{96,64},{112,80},{1... | collective-permute-start | bytes 3194888 | tf_op jit(solution)/shard_map/ppermute | solution.py:431
  57.7 2.9 %collective-permute-done.9.refs_11_.refs_16_ = f32[512,512]{1,0:T(8,128)} collective-permute-done((f32[512,512]{1,0:T(8,128)}, f32[512,512]{1,0:T(8,128)}, u32[]{:S(2)}, u32[]{:S(2)}) %collective-permute-start.9) | collective-permute-done | bytes 1048608 | tf_op jit(solution)/shard_map/ppermute | solution.py:426
  60.7 17.8 %collective-permute-done.8.refs_10_.refs_15_ = f32[512,512]{1,0:T(8,128)S(1)} collective-permute-done((f32[512,512]{1,0:T(8,128)}, f32[512,512]{1,0:T(8,128)S(1)}, u32[]{:S(2)}, u32[]{:S(2)}) %collective-permute-start.8) | collective-permute-done | bytes 1048608 | tf_op jit(solution)/shard_map/ppermute | solution.py:425
  79.5 2.5 %collective-permute-start.13 = (f32[264,512]{1,0:T(8,128)}, f32[264,512]{1,0:T(8,128)}, u32[]{:S(2)}, u32[]{:S(2)}) collective-permute-start(f32[264,512]{1,0:T(8,128)} %collective-permute-done.2.refs_3_), channel_id=1, source_target_pairs={{0,16},{16,0},{32,48},{48,32},{64,80},{80,64},{96,112},{112,96},{1... | collective-permute-start | bytes 1622024 | tf_op jit(solution)/shard_map/ppermute | solution.py:433
  82.1 18.1 %collective-permute-done.15.refs_13_ = f32[512,512]{1,0:T(8,128)S(1)} collective-permute-done((f32[512,512]{1,0:T(8,128)}, f32[512,512]{1,0:T(8,128)S(1)}, u32[]{:S(2)}, u32[]{:S(2)}) %collective-permute-start.15) | collective-permute-done | bytes 1048608 | tf_op jit(solution)/shard_map/ppermute | solution.py:429
  101.1 2.8 %collective-permute-start.14 = (f32[256,512]{1,0:T(8,128)}, f32[256,512]{1,0:T(8,128)}, u32[]{:S(2)}, u32[]{:S(2)}) collective-permute-start(f32[256,512]{1,0:T(8,128)} %copy-done.14), channel_id=1, source_target_pairs={{0,16},{16,0},{32,48},{48,32},{64,80},{80,64},{96,112},{112,96},{1... | collective-permute-start | bytes 1572872 | tf_op jit(solution)/shard_map/ppermute | solution.py:433
  104.0 9.2 %slot_entries.1 = (f32[128,512]{1,0:T(8,128)}, f32[128,512]{1,0:T(8,128)}, f32[128,512]{1,0:T(8,128)}, f32[128,512]{1,0:T(8,128)}, f32[512,512]{1,0:T(8,128)}, /*index=5*/s32[2,256]{1,0:T(2,128)}) custom-call(s32[2,256]{1,0:T(2,128)} %bitcast.12, f32[256,2,512]{2,1,0:T(2,128)} %values.1), custom_call_target="tpu_custom_call" | custom-call | flops 1610612736 | bytes 6291456 | tf_op jit(solution)/shard_map/slot_entries/pallas_call | solution.py:320
  117.9 5.9 %couple_early.1.before = f32[512,512]{1,0:T(8,128)S(1)} custom-call(s32[16,8]{1,0:T(8,128)S(1)} %copy.11.pattern, f32[520,512]{1,0:T(8,128)S(1)} %copy-done, f32[520,512]{1,0:T(8,128)S(1)} %collective-permute-done.refs_1_, f32[520,512]{1,0:T(8,128)S(1)} %collective-permute-done.1.refs_2_, f32[264,512]{1,0:T(8,128)} %collective-permute-done.2.refs_3_, ...), custom_call_target="tpu_custom_call" | custom-call | flops 4026531840 | bytes 11534336 | tf_op jit(solution)/shard_map/couple_early/pallas_call | solution.py:242
  126.0 9.2 %couple_late.1 = f32[640,256]{1,0:T(8,128)S(1)} custom-call(s32[16,8]{1,0:T(8,128)S(1)} %copy.11.pattern, f32[512,512]{1,0:T(8,128)S(1)} %couple_early.1.before, f32[520,512]{1,0:T(8,128)S(1)} %copy-done, f32[520,512]{1,0:T(8,128)} %copy-done.1, f32[520,512]{1,0:T(8,128)} %copy-done.2, f32[264,512]{1,0:T(8,128)} %collective-permute-done.2.refs_3_, ...), custom_call_target="tpu_custom_call" | custom-call | flops 5368709120 | bytes 13631488 | tf_op jit(solution)/shard_map/couple_late/pallas_call | solution.py:257
  135.2 20.8 %all_to_all.21 = f32[16,40,256]{2,1,0:T(8,128)S(1)} all-to-all(f32[16,40,256]{2,1,0:T(8,128)S(1)} %bitcast.8), channel_id=1, replica_groups=mesh['row'=8,'col'=16] {'col'}, dimensions={0} | all-to-all | bytes 1310720 | tf_op jit(solution)/shard_map/all_to_all | solution.py:396
  156.9 8.8 %all-to-all-start.1 = ((f32[16,40,256]{2,1,0:T(8,128)}), f32[16,40,256]{2,1,0:T(8,128)S(1)}, u32[]{:S(2)}, u32[]{:S(2)}) async-start(f32[16,40,256]{2,1,0:T(8,128)} %broadcast_in_dim.2), calls=%async_computation.1 | async-start | bytes 1310720 | tf_op jit(solution)/shard_map/all_to_all | solution.py:396
  166.5 2.9 %collective-permute-start.18 = (f32[128,512]{1,0:T(8,128)S(1)}, f32[128,512]{1,0:T(8,128)S(1)}, u32[]{:S(2)}, u32[]{:S(2)}) collective-permute-start(f32[128,512]{1,0:T(8,128)S(1)} %copy-done.20), channel_id=1, source_target_pairs={{0,64},{16,80},{32,96},{48,112},{64,0},{80,16},{96,32},{112,48},{1... | collective-permute-start | bytes 786440 | tf_op jit(solution)/shard_map/ppermute | solution.py:440
  169.4 2.4 %collective-permute-start.19 = (f32[128,512]{1,0:T(8,128)S(1)}, f32[128,512]{1,0:T(8,128)S(1)}, u32[]{:S(2)}, u32[]{:S(2)}) collective-permute-start(f32[128,512]{1,0:T(8,128)S(1)} %copy-done.19), channel_id=1, source_target_pairs={{0,96},{16,112},{32,0},{48,16},{64,32},{80,48},{96,64},{112,80},{1... | collective-permute-start | bytes 786440 | tf_op jit(solution)/shard_map/ppermute | solution.py:440
  175.6 10.6 %collective-permute-start.21 = (f32[128,512]{1,0:T(8,128)S(1)}, f32[128,512]{1,0:T(8,128)S(1)}, u32[]{:S(2)}, u32[]{:S(2)}) collective-permute-start(f32[128,512]{1,0:T(8,128)S(1)} %get-tuple-element.20), channel_id=1, source_target_pairs={{0,32},{16,48},{32,64},{48,80},{64,96},{80,112},{96,0},{112,16},{1... | collective-permute-start | bytes 786440 | tf_op jit(solution)/shard_map/ppermute | solution.py:442
  189.7 2.9 %collective-permute-done.21.refs_5_ = f32[128,512]{1,0:T(8,128)S(1)} collective-permute-done((f32[128,512]{1,0:T(8,128)S(1)}, f32[128,512]{1,0:T(8,128)S(1)}, u32[]{:S(2)}, u32[]{:S(2)}) %collective-permute-start.21) | collective-permute-done | bytes 262176 | tf_op jit(solution)/shard_map/ppermute | solution.py:442
  193.5 4.8 %forms.1 = (f32[512,512]{1,0:T(8,128)}, f32[8,128]{1,0:T(8,128)}) custom-call(f32[640,256]{1,0:T(8,128)} %bitcast.9, f32[512,512]{1,0:T(8,128)} %d.1, f32[128,512]{1,0:T(8,128)} %get-tuple-element.10.refs_0_, f32[128,512]{1,0:T(8,128)} %copy-done.22, f32[128,512]{1,0:T(8,128)} %copy-done.23, f32[128,512]{1,0:T(8,128)} %copy-done.24, f32[512,512]{1,0:T(8,128)} %copy-done.17, ...), custom_call_target="tpu_custom_call" | custom-call | flops 1610612736 | bytes 5242880 | tf_op jit(solution)/shard_map/forms/pallas_call | solution.py:357
  198.3 14.5 %all_to_all.22 = f32[8,1,128]{2,1,0:T(1,128)} all-to-all(f32[8,1,128]{2,1,0:T(1,128)} %bitcast.11), channel_id=1, replica_groups=mesh['row'=8,'col'=16] {'row'}, dimensions={0} | all-to-all | bytes 8192 | tf_op jit(solution)/shard_map/all_to_all | solution.py:396
  (96 shorter events, 29.2 us)
Async XLA Ops:
  0.6 11.2 %collective-permute-start.10 = (f32[512,512]{1,0:T(8,128)}, f32[512,512]{1,0:T(8,128)}, u32[]{:S(2)}, u32[]{:S(2)}) collective-permute-start(f32[512,512]{1,0:T(8,128)} %refs_10_.1), channel_id=1, source_target_pairs={{0,1},{1,0},{2,3},{3,2},{4,5},{5,4},{6,7},{7,6},{8,9},{9,8},{10,11... | collective-permute-start | bytes 3145736 | tf_op jit(solution)/shard_map/ppermute | solution.py:423
  0.7 25.4 %collective-permute-start.7 = (f32[512,512]{1,0:T(8,128)}, f32[512,512]{1,0:T(8,128)}, u32[]{:S(2)}, u32[]{:S(2)}) collective-permute-start(f32[512,512]{1,0:T(8,128)} %refs_10_.1), channel_id=1, source_target_pairs={{0,8},{1,9},{2,10},{3,11},{4,12},{5,13},{6,14},{7,15},{8,1},{9,0},... | collective-permute-start | bytes 3145736 | tf_op jit(solution)/shard_map/ppermute | solution.py:417
  5.0 28.1 %collective-permute-start = (f32[520,512]{1,0:T(8,128)}, f32[520,512]{1,0:T(8,128)S(1)}, u32[]{:S(2)}, u32[]{:S(2)}) collective-permute-start(f32[520,512]{1,0:T(8,128)} %pick.1.refs_0_), channel_id=1, source_target_pairs={{0,32},{16,48},{32,64},{48,80},{64,96},{80,112},{96,0},{112,16},{1... | collective-permute-start | bytes 3194888 | tf_op jit(solution)/shard_map/ppermute | solution.py:421
  6.9 26.9 %collective-permute-start.1 = (f32[520,512]{1,0:T(8,128)}, f32[520,512]{1,0:T(8,128)S(1)}, u32[]{:S(2)}, u32[]{:S(2)}) collective-permute-start(f32[520,512]{1,0:T(8,128)} %pick.1.refs_0_), channel_id=1, source_target_pairs={{0,96},{16,112},{32,0},{48,16},{64,32},{80,48},{96,64},{112,80},{1... | collective-permute-start | bytes 3194888 | tf_op jit(solution)/shard_map/ppermute | solution.py:422
  9.1 44.5 %collective-permute-start.4 = (f32[520,512]{1,0:T(8,128)}, f32[520,512]{1,0:T(8,128)}, u32[]{:S(2)}, u32[]{:S(2)}) collective-permute-start(f32[520,512]{1,0:T(8,128)} %pick.1.refs_0_), channel_id=1, source_target_pairs={{0,16},{16,0},{32,48},{48,32},{64,80},{80,64},{96,112},{112,96},{1... | collective-permute-start | bytes 3194888 | tf_op jit(solution)/shard_map/ppermute | solution.py:424
  11.9 26.7 %collective-permute-start.6 = (f32[512,512]{1,0:T(8,128)S(1)}, f32[512,512]{1,0:T(8,128)S(1)}, u32[]{:S(2)}, u32[]{:S(2)}) collective-permute-start(f32[512,512]{1,0:T(8,128)S(1)} %copy-done.3), channel_id=1, source_target_pairs={{0,7},{1,6},{2,1},{3,0},{4,3},{5,2},{6,5},{7,4},{8,15},{9,14},{10,... | collective-permute-start | bytes 3145736 | tf_op jit(solution)/shard_map/ppermute | solution.py:419
  26.2 26.1 %collective-permute-start.5 = (f32[512,512]{1,0:T(8,128)S(1)}, f32[512,512]{1,0:T(8,128)}, u32[]{:S(2)}, u32[]{:S(2)}) collective-permute-start(f32[512,512]{1,0:T(8,128)S(1)} %copy-done.3), channel_id=1, source_target_pairs={{0,2},{1,3},{2,4},{3,5},{4,6},{5,7},{6,0},{7,1},{8,10},{9,11},{10,... | collective-permute-start | bytes 3145736 | tf_op jit(solution)/shard_map/ppermute | solution.py:418
  33.1 27.6 %collective-permute-start.9 = (f32[512,512]{1,0:T(8,128)}, f32[512,512]{1,0:T(8,128)}, u32[]{:S(2)}, u32[]{:S(2)}) collective-permute-start(f32[512,512]{1,0:T(8,128)} %collective-permute-done.7.refs_9_.refs_14_), channel_id=1, source_target_pairs={{0,6},{1,7},{2,0},{3,1},{4,2},{5,3},{6,4},{7,5},{8,14},{9,15},{10,... | collective-permute-start | bytes 3145736 | tf_op jit(solution)/shard_map/ppermute | solution.py:426
  33.9 23.8 %collective-permute-start.2 = (f32[264,512]{1,0:T(8,128)S(1)}, f32[264,512]{1,0:T(8,128)}, u32[]{:S(2)}, u32[]{:S(2)}) collective-permute-start(f32[264,512]{1,0:T(8,128)S(1)} %slice.20), channel_id=1, source_target_pairs={{0,32},{16,48},{32,64},{48,80},{64,96},{80,112},{96,0},{112,16},{1... | collective-permute-start | bytes 1622024 | tf_op jit(solution)/shard_map/ppermute | solution.py:428
  39.5 14.1 %collective-permute-start.3 = (f32[256,512]{1,0:T(8,128)S(1)}, f32[256,512]{1,0:T(8,128)S(1)}, u32[]{:S(2)}, u32[]{:S(2)}) collective-permute-start(f32[256,512]{1,0:T(8,128)S(1)} %slice.21), channel_id=1, source_target_pairs={{0,96},{16,112},{32,0},{48,16},{64,32},{80,48},{96,64},{112,80},{1... | collective-permute-start | bytes 1572872 | tf_op jit(solution)/shard_map/ppermute | solution.py:428
  52.2 26.2 %collective-permute-start.8 = (f32[512,512]{1,0:T(8,128)}, f32[512,512]{1,0:T(8,128)S(1)}, u32[]{:S(2)}, u32[]{:S(2)}) collective-permute-start(f32[512,512]{1,0:T(8,128)} %collective-permute-done.7.refs_9_.refs_14_), channel_id=1, source_target_pairs={{0,2},{1,3},{2,4},{3,5},{4,6},{5,7},{6,0},{7,1},{8,10},{9,11},{10,... | collective-permute-start | bytes 3145736 | tf_op jit(solution)/shard_map/ppermute | solution.py:425
  53.6 46.6 %collective-permute-start.15 = (f32[512,512]{1,0:T(8,128)}, f32[512,512]{1,0:T(8,128)S(1)}, u32[]{:S(2)}, u32[]{:S(2)}) collective-permute-start(f32[512,512]{1,0:T(8,128)} %collective-permute-done.5.refs_7_.refs_11_), channel_id=1, source_target_pairs={{0,3},{1,2},{2,4},{3,5},{4,6},{5,7},{6,1},{7,0},{8,11},{9,10},{10,... | collective-permute-start | bytes 3145736 | tf_op jit(solution)/shard_map/ppermute | solution.py:429
  53.6 72.3 %collective-permute-start.12 = (f32[520,512]{1,0:T(8,128)}, f32[520,512]{1,0:T(8,128)}, u32[]{:S(2)}, u32[]{:S(2)}) collective-permute-start(f32[520,512]{1,0:T(8,128)} %collective-permute-done.4.refs_5_), channel_id=1, source_target_pairs={{0,96},{16,112},{32,0},{48,16},{64,32},{80,48},{96,64},{112,80},{1... | collective-permute-start | bytes 3194888 | tf_op jit(solution)/shard_map/ppermute | solution.py:431
  57.7 68.2 %collective-permute-start.11 = (f32[520,512]{1,0:T(8,128)}, f32[520,512]{1,0:T(8,128)}, u32[]{:S(2)}, u32[]{:S(2)}) collective-permute-start(f32[520,512]{1,0:T(8,128)} %collective-permute-done.4.refs_5_), channel_id=1, source_target_pairs={{0,32},{16,48},{32,64},{48,80},{64,96},{80,112},{96,0},{112,16},{1... | collective-permute-start | bytes 3194888 | tf_op jit(solution)/shard_map/ppermute | solution.py:430
  60.7 65.3 %collective-permute-start.16 = (f32[512,512]{1,0:T(8,128)}, f32[512,512]{1,0:T(8,128)}, u32[]{:S(2)}, u32[]{:S(2)}) collective-permute-start(f32[512,512]{1,0:T(8,128)} %collective-permute-done.9.refs_11_.refs_16_), channel_id=1, source_target_pairs={{0,6},{1,7},{2,0},{3,1},{4,2},{5,3},{6,4},{7,5},{8,14},{9,15},{10,... | collective-permute-start | bytes 3145736 | tf_op jit(solution)/shard_map/ppermute | solution.py:432
  79.5 46.4 %collective-permute-start.13 = (f32[264,512]{1,0:T(8,128)}, f32[264,512]{1,0:T(8,128)}, u32[]{:S(2)}, u32[]{:S(2)}) collective-permute-start(f32[264,512]{1,0:T(8,128)} %collective-permute-done.2.refs_3_), channel_id=1, source_target_pairs={{0,16},{16,0},{32,48},{48,32},{64,80},{80,64},{96,112},{112,96},{1... | collective-permute-start | bytes 1622024 | tf_op jit(solution)/shard_map/ppermute | solution.py:433
  101.1 22.7 %collective-permute-start.14 = (f32[256,512]{1,0:T(8,128)}, f32[256,512]{1,0:T(8,128)}, u32[]{:S(2)}, u32[]{:S(2)}) collective-permute-start(f32[256,512]{1,0:T(8,128)} %copy-done.14), channel_id=1, source_target_pairs={{0,16},{16,0},{32,48},{48,32},{64,80},{80,64},{96,112},{112,96},{1... | collective-permute-start | bytes 1572872 | tf_op jit(solution)/shard_map/ppermute | solution.py:433
  123.9 47.9 %collective-permute-start.20 = (f32[512,512]{1,0:T(8,128)}, f32[512,512]{1,0:T(8,128)S(1)}, u32[]{:S(2)}, u32[]{:S(2)}) collective-permute-start(f32[512,512]{1,0:T(8,128)} %get-tuple-element.14), channel_id=1, source_target_pairs={{0,16},{16,0},{32,48},{48,32},{64,80},{80,64},{96,112},{112,96},{1... | collective-permute-start | bytes 3145736 | tf_op jit(solution)/shard_map/ppermute | solution.py:439
  156.9 35.7 %all-to-all-start.1 = ((f32[16,40,256]{2,1,0:T(8,128)}), f32[16,40,256]{2,1,0:T(8,128)S(1)}, u32[]{:S(2)}, u32[]{:S(2)}) async-start(f32[16,40,256]{2,1,0:T(8,128)} %broadcast_in_dim.2), calls=%async_computation.1 | async-start | bytes 1310720 | tf_op jit(solution)/shard_map/all_to_all | solution.py:396
  166.5 19.8 %collective-permute-start.18 = (f32[128,512]{1,0:T(8,128)S(1)}, f32[128,512]{1,0:T(8,128)S(1)}, u32[]{:S(2)}, u32[]{:S(2)}) collective-permute-start(f32[128,512]{1,0:T(8,128)S(1)} %copy-done.20), channel_id=1, source_target_pairs={{0,64},{16,80},{32,96},{48,112},{64,0},{80,16},{96,32},{112,48},{1... | collective-permute-start | bytes 786440 | tf_op jit(solution)/shard_map/ppermute | solution.py:440
  169.4 16.8 %collective-permute-start.19 = (f32[128,512]{1,0:T(8,128)S(1)}, f32[128,512]{1,0:T(8,128)S(1)}, u32[]{:S(2)}, u32[]{:S(2)}) collective-permute-start(f32[128,512]{1,0:T(8,128)S(1)} %copy-done.19), channel_id=1, source_target_pairs={{0,96},{16,112},{32,0},{48,16},{64,32},{80,48},{96,64},{112,80},{1... | collective-permute-start | bytes 786440 | tf_op jit(solution)/shard_map/ppermute | solution.py:440
  171.9 16.4 %collective-permute-start.23 = (f32[128,512]{1,0:T(8,128)S(1)}, f32[128,512]{1,0:T(8,128)S(1)}, u32[]{:S(2)}, u32[]{:S(2)}) collective-permute-start(f32[128,512]{1,0:T(8,128)S(1)} %get-tuple-element.18), channel_id=1, source_target_pairs={{0,96},{16,112},{32,0},{48,16},{64,32},{80,48},{96,64},{112,80},{1... | collective-permute-start | bytes 786440 | tf_op jit(solution)/shard_map/ppermute | solution.py:442
  172.0 16.3 %collective-permute-start.22 = (f32[128,512]{1,0:T(8,128)S(1)}, f32[128,512]{1,0:T(8,128)S(1)}, u32[]{:S(2)}, u32[]{:S(2)}) collective-permute-start(f32[128,512]{1,0:T(8,128)S(1)} %get-tuple-element.19), channel_id=1, source_target_pairs={{0,64},{16,80},{32,96},{48,112},{64,0},{80,16},{96,32},{112,48},{1... | collective-permute-start | bytes 786440 | tf_op jit(solution)/shard_map/ppermute | solution.py:442
  175.6 17.0 %collective-permute-start.21 = (f32[128,512]{1,0:T(8,128)S(1)}, f32[128,512]{1,0:T(8,128)S(1)}, u32[]{:S(2)}, u32[]{:S(2)}) collective-permute-start(f32[128,512]{1,0:T(8,128)S(1)} %get-tuple-element.20), channel_id=1, source_target_pairs={{0,32},{16,48},{32,64},{48,80},{64,96},{80,112},{96,0},{112,16},{1... | collective-permute-start | bytes 786440 | tf_op jit(solution)/shard_map/ppermute | solution.py:442
  (29 other events, 418.7 us)
